TPU v7x, 32 devices: a whole 2x2x4 slice. The times are simulated.
32 devices in a mesh: group: 2 (over y), dp: 8 (over z, x), tensor: 2 (over core).
Axes of the slice: x: 2, y: 2, z: 4, core: 2. Of those that a mesh axis runs over, the one named last changes fastest.
Arguments:
- inputs: bfloat16 [12288, 1536], P(('group', 'dp')), may hold values from -6 to 6
- cotangent: bfloat16 [12288, 1536], P(('group', 'dp')), may hold values from -6 to 6
- lengths: int32 [16, 3], P(('group', 'dp')), may hold values from 1 to 576, 768 in all within a row
- attn_gain: bfloat16 [1536], P('dp'), may hold values from 0.25 to 1.75
- w_query: bfloat16 [1536, 1536], P('dp', 'tensor'), may hold values from -0.15625 to 0.15625
- b_query: bfloat16 [1536], P('tensor'), may hold values from -3 to 3
- w_key: bfloat16 [1536, 256], P('dp', 'tensor'), may hold values from -0.15625 to 0.15625
- b_key: bfloat16 [256], P('tensor'), may hold values from -3 to 3
- w_value: bfloat16 [1536, 256], P('dp', 'tensor'), may hold values from -0.15625 to 0.15625
- b_value: bfloat16 [256], P('tensor'), may hold values from -3 to 3
- w_out: bfloat16 [1536, 1536], P('dp', 'tensor'), may hold values from -1.25 to 1.25
- ffn_gain: bfloat16 [1536], P('dp'), may hold values from 0.25 to 1.75
- w_gate: bfloat16 [1536, 8960], P('dp', 'tensor'), may hold values from -0.15625 to 0.15625
- w_up: bfloat16 [1536, 8960], P('dp', 'tensor'), may hold values from -0.15625 to 0.15625
- w_down: bfloat16 [1536, 8960], P('dp', 'tensor'), may hold values from -0.0625 to 0.0625
Outputs:
- layer_out: bfloat16 [12288, 1536], P(('group', 'dp'))
- input_grad: bfloat16 [12288, 1536], P(('group', 'dp'))
- attn_gain_grad: float32 [1536], P('dp')
- w_query_grad: float32 [1536, 1536], P('dp', 'tensor')
- b_query_grad: float32 [1536], P('tensor')
- w_key_grad: float32 [1536, 256], P('dp', 'tensor')
- b_key_grad: float32 [256], P('tensor')
- w_value_grad: float32 [1536, 256], P('dp', 'tensor')
- b_value_grad: float32 [256], P('tensor')
- w_out_grad: float32 [1536, 1536], P('dp', 'tensor')
- ffn_gain_grad: float32 [1536], P('dp')
- w_gate_grad: float32 [1536, 8960], P('dp', 'tensor')
- w_up_grad: float32 [1536, 8960], P('dp', 'tensor')
- w_down_grad: float32 [1536, 8960], P('dp', 'tensor')
Inputs may be any that keep to these rules, and one draw needn't show every extreme that they name: In every stream the 3 lengths sum to 768, and the longest is exactly 576.
All inputs are finite; a program needn't handle non-finite values.
Results may differ from a plain program's by a relative error of at most 0.017.
Values may be sent and summed in bfloat16 or wider, within the bound.
No kernel may reach another device: no remote copies, remote signals or barrier semaphores. Data moves between devices by JAX's collectives and lax.ppermute only.
A program may use at most 384 MiB of HBM per device.

v0:
```python
import math
import jax
import jax.numpy as jnp
from jax import lax
from jax.sharding import PartitionSpec as P

HD = 128
SEQ = 768
NSEG = 3
EPSILON = 1e-06
THETA = 10000.0
MASKED_SCORE = -1e30


def normalize(values):
    return values * lax.rsqrt(jnp.mean(values * values, axis=-1, keepdims=True) + EPSILON)


def scaled_norm(values, gain_vec):
    return normalize(values) * gain_vec


def rotate(values, cosine, sine_table):
    half_width = values.shape[-1] // 2
    turned = jnp.concatenate([-values[..., half_width:], values[..., :half_width]], axis=-1)
    return values * cosine + turned * sine_table


def unrotate(values, cosine, sine_table):
    half_width = values.shape[-1] // 2
    sined = values * sine_table
    turned = jnp.concatenate([sined[..., half_width:], -sined[..., :half_width]], axis=-1)
    return values * cosine + turned


def layout(lengths):
    segment_ends = jnp.cumsum(lengths, axis=-1)
    segment_starts = segment_ends - lengths
    places = jnp.arange(SEQ, dtype=jnp.int32)
    segment = jnp.sum((places[:, None] >= segment_ends[..., None, :]).astype(jnp.int32), axis=-1)
    choose = segment[..., None] == jnp.arange(NSEG, dtype=jnp.int32)
    picked = jnp.sum(jnp.where(choose, segment_starts[..., None, :], 0), axis=-1)
    return (segment, places - picked)


def angles(position):
    frequency = jnp.exp(-(math.log(THETA) * 2.0 / HD) * jnp.arange(HD // 2, dtype=jnp.float32))
    phase_angle = position.astype(jnp.float32)[..., None] * frequency
    phase_angle = jnp.concatenate([phase_angle, phase_angle], axis=-1)
    return (jnp.cos(phase_angle), jnp.sin(phase_angle))


def plain_dot(left_side, right_side):
    return jnp.dot(left_side, right_side, preferred_element_type=jnp.float32)


def trans_dot(left_side, right_side):
    return lax.dot_general(
        left_side, right_side, (((1,), (1,)), ((), ())), preferred_element_type=jnp.float32
    )


def outer_dot(left_side, right_side):
    return lax.dot_general(
        left_side, right_side, (((0,), (0,)), ((), ())), preferred_element_type=jnp.float32
    )


def masked_scores(queries, keys_rot, allowed):
    raw_scores = jnp.einsum("qkgd,skd->kgqs", queries, keys_rot, preferred_element_type=jnp.float32)
    return jnp.where(allowed, raw_scores * HD ** (-0.5), MASKED_SCORE)


AXES = ("group", "dp", "tensor")


def routes(dp_count):

    def table(move):
        flat = lambda g, d, t: (g * dp_count + d) * 2 + t
        return [
            (flat(g, d, t), flat(*move(g, d, t)))
            for g in range(2)
            for d in range(dp_count)
            for t in range(2)
        ]

    return {
        "x": table(lambda g, d, t: (g, d ^ 1, t)),
        "y": table(lambda g, d, t: (g ^ 1, d, t)),
        "t": table(lambda g, d, t: (g, d, t ^ 1)),
        "first": table(lambda g, d, t: (g, d ^ 1, t) if t == 0 else (g ^ 1, d, t)),
        "second": table(lambda g, d, t: (g ^ 1, d, t) if t == 0 else (g, d ^ 1, t)),
    }


def local(
    inputs,
    cotangent,
    lengths,
    attn_gain,
    w_query,
    b_query,
    w_key,
    b_key,
    w_value,
    b_value,
    w_out,
    ffn_gain,
    w_gate,
    w_up,
    w_down,
):
    bf16 = jnp.bfloat16
    f32 = jnp.float32
    dp_count = lax.axis_size("dp")
    line = dp_count // 2
    dp_index = lax.axis_index("dp")
    x_index = dp_index % 2
    y_index = lax.axis_index("group")
    core = lax.axis_index("tensor")
    table = routes(dp_count)
    line_groups = [[2 * z + x for z in range(line)] for x in range(2)]
    tokens, d_model = inputs.shape
    half = tokens // 2
    rows = w_query.shape[0]
    head_count = w_query.shape[1] // HD
    kv_count = w_key.shape[1] // HD
    group_size = head_count // kv_count
    ffn_cols = w_gate.shape[1]
    quarter = -(-ffn_cols // 512) * 128
    score_scale = HD ** (-0.5)

    def send(value, route):
        return lax.ppermute(value, AXES, table[route])

    def pick(value, index):
        return lax.dynamic_index_in_dim(value, index, 0, keepdims=False)

    def in_order(index, mine, other):
        first = index == 0
        return (jnp.where(first, mine, other), jnp.where(first, other, mine))

    def my_half(value):
        return pick(value.reshape(2, half, value.shape[-1]), core)

    def other_half(value):
        return pick(value.reshape(2, half, value.shape[-1]), 1 - core)

    def both_halves(mine):
        return jnp.concatenate(in_order(core, mine, send(mine, "t")), axis=0)

    def square_gather(mine):
        near = send(mine, "first")
        mine_sib = send(mine, "t")
        far = send(jnp.stack([mine, near]), "second")
        near_sib = send(near, "t")
        far_sib = send(far, "t")
        return jnp.concatenate(
            [mine, near, far[0], far[1], mine_sib, near_sib, far_sib[0], far_sib[1]], axis=0
        )

    def square_scatter(mine, theirs):
        came = send(theirs.astype(bf16), "t")
        total = (mine.astype(f32) + came.astype(f32)).reshape(4, half, d_model)
        came = send(total[2:].astype(bf16), "second")
        total = total[:2] + came.astype(f32)
        came = send(total[1].astype(bf16), "first")
        return total[0] + came.astype(f32)

    def ffn_gather(weight):
        padded = jnp.pad(weight, ((0, 0), (0, 4 * quarter - ffn_cols)))
        parts = padded.reshape(rows, 4, quarter).transpose(1, 0, 2)
        mine = pick(parts, x_index * 2 + y_index)
        came = send(pick(parts, (1 - x_index) * 2 + y_index), "x")
        pair = jnp.stack(in_order(x_index, mine, came))
        full = lax.all_gather(pair, "dp", axis=0, axis_index_groups=line_groups)
        return full.reshape(d_model, quarter)

    def ffn_scatter(grad):
        parts = grad.astype(bf16).reshape(line, 2 * rows, quarter)
        summed = lax.psum_scatter(
            parts, "dp", scatter_dimension=0, axis_index_groups=line_groups
        ).reshape(2, rows, quarter)
        came = send(pick(summed, 1 - x_index), "x")
        pair = jnp.stack(in_order(x_index, pick(summed, x_index), came))
        low, high = in_order(y_index, pair, send(pair, "y"))
        whole = jnp.concatenate([low[0], high[0], low[1], high[1]], axis=1)
        return whole[:, :ffn_cols].astype(f32)

    def attn_scatter(grad):
        summed = lax.psum_scatter(grad.astype(bf16), "dp", scatter_dimension=0, tiled=True)
        return summed.astype(f32) + send(summed, "y").astype(f32)

    stream = inputs.astype(f32)
    segment, position = layout(lengths[0])
    cosine, sine_table = angles(position)
    cosine = cosine[:, None, :]
    sine_table = sine_table[:, None, :]
    places = jnp.arange(SEQ, dtype=jnp.int32)
    allowed = (segment[:, None] == segment[None, :]) & (places[None, :] <= places[:, None])
    gains = jnp.pad(jnp.stack([attn_gain, ffn_gain], axis=1), ((0, 0), (0, 126)))
    query_cols = head_count * HD
    key_cols = kv_count * HD
    qkv_cols = query_cols + 2 * key_cols
    qkv_full = lax.all_gather(
        jnp.concatenate([w_query, w_key, w_value, gains], axis=1), "dp", axis=0, tiled=True
    )
    out_full = lax.all_gather(w_out, "dp", axis=0, tiled=True)
    gate_full = ffn_gather(w_gate)
    up_full = ffn_gather(w_up)
    down_full = ffn_gather(w_down)
    cot_half = my_half(cotangent)
    cot_all = square_gather(cot_half)
    gain_one = qkv_full[:, qkv_cols].astype(f32)
    gain_two = qkv_full[:, qkv_cols + 1].astype(f32)
    qkv_full = qkv_full[:, :qkv_cols]
    inv_one = lax.rsqrt(jnp.mean(stream * stream, axis=-1, keepdims=True) + EPSILON)
    h_one = (stream * inv_one * gain_one).astype(bf16)
    qkv_bias = jnp.concatenate([b_query, b_key, b_value]).astype(f32)
    qkv_pre = plain_dot(h_one, qkv_full) + qkv_bias
    query_pre = qkv_pre[:, :query_cols]
    key_pre = qkv_pre[:, query_cols : query_cols + key_cols]
    value_pre = qkv_pre[:, query_cols + key_cols :]
    queries = rotate(query_pre.reshape(SEQ, head_count, HD), cosine, sine_table).astype(bf16)
    queries = queries.reshape(SEQ, kv_count, group_size, HD)
    keys_rot = rotate(key_pre.reshape(SEQ, kv_count, HD), cosine, sine_table).astype(bf16)
    values_low = value_pre.astype(bf16).reshape(SEQ, kv_count, HD)
    scores = masked_scores(queries, keys_rot, allowed)
    row_max = jnp.max(scores, axis=-1, keepdims=True)
    exp_terms = jnp.exp(scores - row_max)
    row_total = jnp.sum(exp_terms, axis=-1, keepdims=True)
    log_total = row_max + jnp.log(row_total)
    probs_low = (exp_terms / row_total).astype(bf16)
    attended = jnp.einsum("kgqs,skd->qkgd", probs_low, values_low, preferred_element_type=f32)
    attended = attended.reshape(SEQ, head_count * HD).astype(bf16)
    branch = trans_dot(attended, out_full)
    resid = (
        my_half(stream) + my_half(branch) + send(other_half(branch).astype(bf16), "t").astype(f32)
    )
    inv_two = lax.rsqrt(jnp.mean(resid * resid, axis=-1, keepdims=True) + EPSILON)
    norm_two = resid * inv_two
    h_two = square_gather((norm_two * gain_two).astype(bf16))
    gate_pre = plain_dot(h_two, gate_full)
    up_pre = plain_dot(h_two, up_full)
    sigmoid_gate = jax.nn.sigmoid(gate_pre)
    swish_gate = gate_pre * sigmoid_gate
    hidden = (swish_gate * up_pre).astype(bf16)
    down_grad = ffn_scatter(outer_dot(cot_all, hidden))
    d_hidden = plain_dot(cot_all, down_full)
    d_gate = (d_hidden * up_pre * sigmoid_gate * (1.0 + gate_pre * (1.0 - sigmoid_gate))).astype(
        bf16
    )
    d_up = (d_hidden * swish_gate).astype(bf16)
    mid = 4 * half

    def entry(part):
        return trans_dot(d_gate[part], gate_full) + trans_dot(d_up[part], up_full)

    d_h_two = square_scatter(entry(slice(0, mid)), entry(slice(mid, None)))
    gate_grad = ffn_scatter(outer_dot(h_two, d_gate))
    up_grad = ffn_scatter(outer_dot(h_two, d_up))
    ffn_total = square_scatter(
        trans_dot(hidden[:mid], down_full), trans_dot(hidden[mid:], down_full)
    )
    layer_out = both_halves((resid + ffn_total).astype(bf16))
    scaled = d_h_two * gain_two
    d_resid = cot_half.astype(f32) + inv_two * (
        scaled - norm_two * jnp.mean(norm_two * scaled, axis=-1, keepdims=True)
    )
    gain_two_part = jnp.sum(d_h_two * norm_two, axis=0)
    d_out_low = both_halves(d_resid.astype(bf16))
    out_grad = attn_scatter(outer_dot(d_out_low, attended))
    d_attended = plain_dot(d_out_low, out_full).astype(bf16).reshape(SEQ, kv_count, group_size, HD)
    scores = masked_scores(queries, keys_rot, allowed)
    probabilities = jnp.exp(scores - log_total)
    d_probs = jnp.einsum("qkgd,skd->kgqs", d_attended, values_low, preferred_element_type=f32)
    d_value = jnp.einsum(
        "kgqs,qkgd->skd", probabilities.astype(bf16), d_attended, preferred_element_type=f32
    )
    d_value = d_value.reshape(SEQ, kv_count * HD).astype(bf16)
    d_scores = probabilities * (d_probs - jnp.sum(probabilities * d_probs, axis=-1, keepdims=True))
    d_scores = d_scores.astype(bf16)
    d_query_rot = (
        jnp.einsum("kgqs,skd->qkgd", d_scores, keys_rot, preferred_element_type=f32) * score_scale
    )
    d_key_rot = (
        jnp.einsum("kgqs,qkgd->skd", d_scores, queries, preferred_element_type=f32) * score_scale
    )
    d_query = (
        unrotate(d_query_rot.reshape(SEQ, head_count, HD), cosine, sine_table)
        .astype(bf16)
        .reshape(SEQ, head_count * HD)
    )
    d_key = unrotate(d_key_rot, cosine, sine_table).astype(bf16).reshape(SEQ, kv_count * HD)
    d_qkv = jnp.concatenate([d_query, d_key, d_value], axis=1)
    qkv_grad = attn_scatter(outer_dot(h_one, d_qkv))
    entry_one = trans_dot(d_qkv, qkv_full)
    d_h_one = my_half(entry_one) + send(other_half(entry_one).astype(bf16), "t").astype(f32)
    half_inv = my_half(inv_one)
    norm_one = my_half(stream) * half_inv
    scaled = d_h_one * gain_one
    input_grad = both_halves(
        (
            d_resid
            + half_inv * (scaled - norm_one * jnp.mean(norm_one * scaled, axis=-1, keepdims=True))
        ).astype(bf16)
    )
    gain_one_part = jnp.sum(d_h_one * norm_one, axis=0)
    bias_part = jnp.sum(d_qkv.astype(f32), axis=0)
    small = jnp.concatenate([gain_one_part, gain_two_part, bias_part]).reshape(-1, 128)
    small = small + send(small, "y")
    step = 1
    while step < dp_count:
        small = small + lax.ppermute(small, "dp", [(i, i ^ step) for i in range(dp_count)])
        step *= 2
    small = small.reshape(-1)
    gain_sums = small[: 2 * d_model].reshape(2, dp_count, rows)
    mine = lax.dynamic_index_in_dim(gain_sums, dp_index, 1, keepdims=False)
    mine = mine + send(mine, "t")
    bias_sum = small[2 * d_model :]
    return (
        layer_out,
        input_grad,
        mine[0],
        qkv_grad[:, :query_cols],
        bias_sum[:query_cols],
        qkv_grad[:, query_cols : query_cols + key_cols],
        bias_sum[query_cols : query_cols + key_cols],
        qkv_grad[:, query_cols + key_cols :],
        bias_sum[query_cols + key_cols :],
        out_grad,
        mine[1],
        gate_grad,
        up_grad,
        down_grad,
    )


def solution(mesh):
    in_specs = (
        P(("group", "dp"), None),
        P(("group", "dp"), None),
        P(("group", "dp"), None),
        P("dp"),
        P("dp", "tensor"),
        P("tensor"),
        P("dp", "tensor"),
        P("tensor"),
        P("dp", "tensor"),
        P("tensor"),
        P("dp", "tensor"),
        P("dp"),
        P("dp", "tensor"),
        P("dp", "tensor"),
        P("dp", "tensor"),
    )
    out_specs = (
        P(("group", "dp"), None),
        P(("group", "dp"), None),
        P("dp"),
        P("dp", "tensor"),
        P("tensor"),
        P("dp", "tensor"),
        P("tensor"),
        P("dp", "tensor"),
        P("tensor"),
        P("dp", "tensor"),
        P("dp"),
        P("dp", "tensor"),
        P("dp", "tensor"),
        P("dp", "tensor"),
    )
    return jax.shard_map(local, mesh=mesh, in_specs=in_specs, out_specs=out_specs, check_vma=False)
```

profile of v0, /device:TPU:0, one launch (start us, length us, event | category | flops | bytes accessed | tf_op | source)
XLA Modules:
  0.0 870.4 jit_solution(2815979763971457537)
XLA Ops:
  17.0 6.6 constant_dynamic-slice_fusion.4
  26.7 11.8 %collective-permute-done.7 = bf16[192,1152]{1,0:T(8,128)(2,1)S(1)} collective-permute-done((bf16[192,1152]{1,0:T(8,128)(2,1)S(1)}, bf16[192,1152]{1,0:T(8,128)(2,1)S(1)}, u32[]{:S(2)}, u32[]{:S(2)}) %collective-permute-start.7) | collective-permute-done | bytes 442400 | tf_op jit(solution)/shard_map/ppermute | solution.py:135
  52.6 14.3 %collective-permute-done.6 = bf16[192,1152]{1,0:T(8,128)(2,1)} collective-permute-done((bf16[192,1152]{1,0:T(8,128)(2,1)}, bf16[192,1152]{1,0:T(8,128)(2,1)}, u32[]{:S(2)}, u32[]{:S(2)}) %collective-permute-start.6) | collective-permute-done | bytes 442400 | tf_op jit(solution)/shard_map/ppermute | solution.py:135
  69.3 22.2 %all-gather.9.cloned.1.call-done = bf16[1536,1152]{1,0:T(8,128)(2,1)} async-done(((bf16[192,1152]{1,0:T(8,128)(2,1)}), bf16[1536,1152]{1,0:T(8,128)(2,1)}) %all-gather.9.cloned.1.call-update) | async-done | bytes 3538960 | tf_op jit(solution)/shard_map/all_gather | solution.py:206
  93.2 4.5 fusion.41
  111.3 3.5 add_convert_fusion.3
  116.2 4.1 fusion.104
  125.6 4.7 fusion.44
  130.3 3.2 convert_element_type.249
  133.5 10.9 %all-gather.11.cloned.1.call-done = bf16[1536,768]{1,0:T(8,128)(2,1)} async-done(((bf16[192,768]{1,0:T(8,128)(2,1)}), bf16[1536,768]{1,0:T(8,128)(2,1)}) %all-gather.11.cloned.1.call-update) | async-done | bytes 2359312 | tf_op jit(solution)/shard_map/all_gather | solution.py:209
  144.4 3.7 fusion.35
  158.3 6.8 collective-permute-done.8
  165.2 26.8 %collective-permute-done.14 = bf16[2,384,1536]{2,1,0:T(8,128)(2,1)} collective-permute-done((bf16[2,384,1536]{2,1,0:T(8,128)(2,1)S(1)}, bf16[2,384,1536]{2,1,0:T(8,128)(2,1)}, u32[]{:S(2)}, u32[]{:S(2)}) %collective-permute-start.14) | collective-permute-done | bytes 2359328 | tf_op jit(solution)/shard_map/ppermute | solution.py:135
  192.0 9.2 %collective-permute-start.17 = (bf16[2,384,1536]{2,1,0:T(8,128)(2,1)}, bf16[2,384,1536]{2,1,0:T(8,128)(2,1)}, u32[]{:S(2)}, u32[]{:S(2)}) collective-permute-start(bf16[2,384,1536]{2,1,0:T(8,128)(2,1)} %collective-permute-done.14), channel_id=1, source_target_pairs={{0,1},{1,0},{2,3},{3,2},{4,5},{5,4},{6,7},{7,6},{8,9},{9,8},{10,11... | collective-permute-start | bytes 7077896 | tf_op jit(solution)/shard_map/ppermute | solution.py:135
  215.9 15.6 %collective-permute-done.2 = bf16[2,384,1536]{2,1,0:T(8,128)(2,1)S(1)} collective-permute-done((bf16[2,384,1536]{2,1,0:T(8,128)(2,1)S(1)}, bf16[2,384,1536]{2,1,0:T(8,128)(2,1)S(1)}, u32[]{:S(2)}, u32[]{:S(2)}) %collective-permute-start.2) | collective-permute-done | bytes 2359328 | tf_op jit(solution)/shard_map/ppermute | solution.py:135
  242.7 17.9 %fusion.106 = f32[3072,1152]{1,0:T(8,128)} fusion(bf16[3072,1536]{1,0:T(8,128)(2,1)} %fusion.60, bf16[1536,1152]{1,0:T(8,128)(2,1)} %bitcast.411), kind=kOutput, calls=%fused_computation.271 | convolution fusion | flops 10871635968 | bytes 27131904 | tf_op jit(solution)/shard_map/dot_general | solution.py:54
  260.6 24.4 %all-gather.13.cloned.1.call-done = bf16[8,192,1152]{2,1,0:T(8,128)(2,1)} async-done(((bf16[2,192,1152]{2,1,0:T(8,128)(2,1)}), bf16[8,192,1152]{2,1,0:T(8,128)(2,1)}) %all-gather.13.cloned.1.call-update) | async-done | bytes 3538960 | tf_op jit(solution)/shard_map/all_gather | solution.py:177
  285.0 17.9 %fusion.105 = f32[3072,1152]{1,0:T(8,128)} fusion(bf16[3072,1536]{1,0:T(8,128)(2,1)} %fusion.60, bf16[1536,1152]{1,0:T(8,128)(2,1)} %bitcast.414), kind=kOutput, calls=%fused_computation.270 | convolution fusion | flops 10871635968 | bytes 27131904 | tf_op jit(solution)/shard_map/dot_general | solution.py:54
  302.9 52.7 %all-gather.17.cloned.1.call-done = bf16[8,192,1152]{2,1,0:T(8,128)(2,1)} async-done(((bf16[2,192,1152]{2,1,0:T(8,128)(2,1)}), bf16[8,192,1152]{2,1,0:T(8,128)(2,1)}) %all-gather.17.cloned.1.call-update) | async-done | bytes 3538960 | tf_op jit(solution)/shard_map/all_gather | solution.py:177
  355.6 29.6 %multiply_convert_fusion = (bf16[3072,1152]{1,0:T(8,128)(2,1)}, bf16[3072,1152]{1,0:T(8,128)(2,1)}, bf16[3072,1152]{1,0:T(8,128)(2,1)}) fusion(f32[3072,1152]{1,0:T(8,128)} %fusion.105, f32[3072,1152]{1,0:T(8,128)} %fusion.106, bf16[3072,1536]{1,0:T(8,128)(2,1)} %fusion.56, bf16[1536,1152]{1,0:T(8,128)(2,1)} %bitcast.417), kind=kOutput, calls=%fused_computation.7 | convolution fusion | flops 10924720128 | bytes 62521344 | tf_op jit(solution)/shard_map/dot_general | solution.py:54
  385.2 18.1 %convolution_convert_fusion.1 = bf16[1536,1152]{1,0:T(8,128)(2,1)} fusion(bf16[3072,1536]{1,0:T(8,128)(2,1)} %fusion.56, bf16[3072,1152]{1,0:T(8,128)(2,1)} %get-tuple-element.30), kind=kOutput, calls=%fused_computation.20 | convolution fusion | flops 10873405440 | bytes 20054016 | tf_op jit(solution)/shard_map/dot_general | solution.py:64
  403.3 18.0 %convolution_convert_fusion.2 = bf16[1536,1152]{1,0:T(8,128)(2,1)} fusion(bf16[3072,1536]{1,0:T(8,128)(2,1)} %fusion.60, bf16[3072,1152]{1,0:T(8,128)(2,1)} %get-tuple-element.28), kind=kOutput, calls=%fused_computation.21 | convolution fusion | flops 10873405440 | bytes 20054016 | tf_op jit(solution)/shard_map/dot_general | solution.py:64
  421.4 10.9 %convolution_convert_fusion = bf16[1536,1536]{1,0:T(8,128)(2,1)} fusion(bf16[1536,1152]{1,0:T(8,128)(2,1)} %bitcast.418, bf16[3072,1152]{1,0:T(8,128)(2,1)} %get-tuple-element.30), kind=kOutput, calls=%fused_computation.19 | convolution fusion | flops 5438177280 | bytes 11796480 | tf_op jit(solution)/shard_map/dot_general | solution.py:58
  432.3 11.0 %fusion.14 = f32[1536,1536]{1,0:T(8,128)} fusion(bf16[1536,1152]{1,0:T(8,128)(2,1)S(1)} %bitcast.416, bf16[3072,1152]{1,0:T(8,128)(2,1)} %get-tuple-element.29), kind=kOutput, calls=%fused_computation.37 | convolution fusion | flops 5435817984 | bytes 16515072 | tf_op jit(solution)/shard_map/dot_general | solution.py:58
  443.3 11.6 %add_convert_fusion = bf16[1536,1536]{1,0:T(8,128)(2,1)} fusion(f32[1536,1536]{1,0:T(8,128)} %fusion.14, bf16[1536,1152]{1,0:T(8,128)(2,1)S(1)} %bitcast.413, bf16[3072,1152]{1,0:T(8,128)(2,1)} %get-tuple-element.28), kind=kOutput, calls=%fused_computation.17 | convolution fusion | flops 5440536576 | bytes 21233664 | tf_op jit(solution)/shard_map/dot_general | solution.py:58
  455.4 14.6 %convolution_convert_fusion.3 = bf16[1536,1152]{1,0:T(8,128)(2,1)} fusion(bf16[3072,1536]{1,0:T(8,128)(2,1)S(1)} %bitcast.406, bf16[3072,1152]{1,0:T(8,128)(2,1)S(1)} %bitcast.422), kind=kOutput, calls=%fused_computation.22 | convolution fusion | flops 10873405440 | bytes 20054016 | tf_op jit(solution)/shard_map/dot_general | solution.py:64
  470.7 12.0 %fusion.17 = f32[1536,1536]{1,0:T(8,128)} fusion(bf16[1536,1152]{1,0:T(8,128)(2,1)} %bitcast.415, bf16[3072,1152]{1,0:T(8,128)(2,1)} %get-tuple-element.29), kind=kOutput, calls=%fused_computation.40 | convolution fusion | flops 5435817984 | bytes 16515072 | tf_op jit(solution)/shard_map/dot_general | solution.py:58
  482.7 8.7 %convert_add_fusion.1 = f32[1536,1536]{1,0:T(8,128)S(1)} fusion(bf16[1536,1536]{1,0:T(8,128)(2,1)} %collective-permute-done.9, bf16[1536,1152]{1,0:T(8,128)(2,1)S(1)} %bitcast.419, bf16[3072,1152]{1,0:T(8,128)(2,1)} %get-tuple-element.30), kind=kOutput, calls=%fused_computation.18 | convolution fusion | flops 5440536576 | bytes 21233664 | tf_op jit(solution)/shard_map/dot_general | solution.py:58
  494.6 12.3 %convert_add_fusion = f32[1536,1536]{1,0:T(8,128)S(1)} fusion(bf16[1536,1536]{1,0:T(8,128)(2,1)} %collective-permute-done.18, f32[1536,1536]{1,0:T(8,128)} %fusion.17, bf16[1536,1152]{1,0:T(8,128)(2,1)} %bitcast.412, bf16[3072,1152]{1,0:T(8,128)(2,1)} %get-tuple-element.28), kind=kOutput, calls=%fused_computation.16 | convolution fusion | flops 5442895872 | bytes 30670848 | tf_op jit(solution)/shard_map/dot_general | solution.py:58
  515.3 22.2 %reduce-scatter.12.cloned.1.call-done = bf16[1,384,1152]{2,1,0:T(8,128)(2,1)} async-done(((bf16[4,384,1152]{2,1,0:T(8,128)(2,1)}), bf16[1,384,1152]{2,1,0:T(8,128)(2,1)}) %reduce-scatter.12.cloned.1.call-update) | async-done | bytes 884752 | tf_op jit(solution)/shard_map/reduce_scatter | solution.py:182
  540.1 66.4 %reduce-scatter.10.cloned.1.call-done = bf16[1,384,1152]{2,1,0:T(8,128)(2,1)} async-done(((bf16[4,384,1152]{2,1,0:T(8,128)(2,1)}), bf16[1,384,1152]{2,1,0:T(8,128)(2,1)}) %reduce-scatter.10.cloned.1.call-update) | async-done | bytes 884752 | tf_op jit(solution)/shard_map/reduce_scatter | solution.py:182
  609.2 4.1 convert_add_fusion.3
  622.5 22.0 %collective-permute-done.20 = bf16[384,1536]{1,0:T(8,128)(2,1)S(1)} collective-permute-done((bf16[384,1536]{1,0:T(8,128)(2,1)S(1)}, bf16[384,1536]{1,0:T(8,128)(2,1)S(1)}, u32[]{:S(2)}, u32[]{:S(2)}) %collective-permute-start.20) | collective-permute-done | bytes 1179680 | tf_op jit(solution)/shard_map/ppermute | solution.py:135
  645.3 3.3 fusion.98
  648.6 14.7 %collective-permute-start.21 = (bf16[384,1536]{1,0:T(8,128)(2,1)S(1)}, bf16[384,1536]{1,0:T(8,128)(2,1)S(1)}, u32[]{:S(2)}, u32[]{:S(2)}) collective-permute-start(bf16[384,1536]{1,0:T(8,128)(2,1)S(1)} %get-tuple-element.20), channel_id=1, source_target_pairs={{0,1},{1,0},{2,3},{3,2},{4,5},{5,4},{6,7},{7,6},{8,9},{9,8},{10,11... | collective-permute-start | bytes 3538952 | tf_op jit(solution)/shard_map/ppermute | solution.py:135
  670.1 8.8 %collective-permute-done.32 = bf16[2,192,1152]{2,1,0:T(8,128)(2,1)S(1)} collective-permute-done((bf16[2,192,1152]{2,1,0:T(8,128)(2,1)S(1)}, bf16[2,192,1152]{2,1,0:T(8,128)(2,1)S(1)}, u32[]{:S(2)}, u32[]{:S(2)}) %collective-permute-start.32) | collective-permute-done | bytes 884768 | tf_op jit(solution)/shard_map/ppermute | solution.py:135
  682.9 3.5 convolution_convert_fusion.5
  686.4 4.4 convolution_convert_fusion.6
  690.9 12.0 %fusion = (f32[6,768]{1,0:T(8,128)S(1)}, f32[768,768,6]{1,0,2:T(8,128)}) fusion(f32[1,6,768,768]{2,3,1,0:T(8,128)} %copy-done, f32[6,768]{1,0:T(8,128)S(1)} %log_add_fusion, bf16[768,6,128]{0,2,1:T(8,128)(2,1)S(1)} %bitcast.387, f32[768,1024]{1,0:T(8,128)} %copy-done.10), kind=kOutput, calls=%fused_computation.3 | convolution fusion | flops 916581888 | bytes 29724672 | tf_op jit(solution)/shard_map/qkgd,skd->kgqs/dot_general | solution.py:277
  705.4 7.8 fusion.9
  713.3 3.2 sine_multiply_fusion
  720.6 4.4 bitcast_multiply_fusion.1
  731.1 5.5 convolution_convert_fusion.4
  736.6 5.1 fusion.24
  741.9 18.4 %collective-permute-start.22 = (bf16[384,1536]{1,0:T(8,128)(2,1)S(1)}, bf16[384,1536]{1,0:T(8,128)(2,1)S(1)}, u32[]{:S(2)}, u32[]{:S(2)}) collective-permute-start(bf16[384,1536]{1,0:T(8,128)(2,1)S(1)} %fusion.53), channel_id=1, source_target_pairs={{0,1},{1,0},{2,3},{3,2},{4,5},{5,4},{6,7},{7,6},{8,9},{9,8},{10,11... | collective-permute-start | bytes 3538952 | tf_op jit(solution)/shard_map/ppermute | solution.py:135
  768.0 3.2 collective-permute-done.25
  784.6 66.6 %reduce-scatter.6.cloned.1.call-done = bf16[192,1024]{1,0:T(8,128)(2,1)} async-done(((bf16[1536,1024]{1,0:T(8,128)(2,1)}), bf16[192,1024]{1,0:T(8,128)(2,1)}) %reduce-scatter.6.cloned.1.call-update) | async-done | bytes 393232 | tf_op jit(solution)/shard_map/reduce_scatter | solution.py:192
  855.0 6.4 collective-permute-done.29
  (373 shorter events, 164.9 us)
Async XLA Ops:
  7.2 84.4 %all-gather.9.cloned.1.call-start = ((), (), s32[]{:S(2)}) async-start(), calls=%async_computation.5 | async-start | bytes 3981312 | tf_op jit(solution)/shard_map/all_gather | solution.py:206
  10.6 133.9 %all-gather.11.cloned.1.call-start = ((), (), s32[]{:S(2)}) async-start(), calls=%async_computation.6 | async-start | bytes 2654208 | tf_op jit(solution)/shard_map/all_gather | solution.py:209
  11.3 231.4 %all-gather.15.cloned.1.call-start = ((), (), s32[]{:S(2)}) async-start(), calls=%async_computation.13 | async-start | bytes 4423680 | tf_op jit(solution)/shard_map/all_gather | solution.py:177
  23.6 14.8 %collective-permute-start.7 = (bf16[192,1152]{1,0:T(8,128)(2,1)S(1)}, bf16[192,1152]{1,0:T(8,128)(2,1)S(1)}, u32[]{:S(2)}, u32[]{:S(2)}) collective-permute-start(bf16[192,1152]{1,0:T(8,128)(2,1)S(1)} %bitcast.404), channel_id=1, source_target_pairs={{0,2},{1,3},{2,0},{3,1},{4,6},{5,7},{6,4},{7,5},{8,10},{9,11},{10,... | collective-permute-start | bytes 1327112 | tf_op jit(solution)/shard_map/ppermute | solution.py:135
  39.6 245.4 %all-gather.13.cloned.1.call-start = ((), (), s32[]{:S(2)}) async-start(), calls=%async_computation.12 | async-start | bytes 4423680 | tf_op jit(solution)/shard_map/all_gather | solution.py:177
  44.5 22.4 %collective-permute-start.6 = (bf16[192,1152]{1,0:T(8,128)(2,1)}, bf16[192,1152]{1,0:T(8,128)(2,1)}, u32[]{:S(2)}, u32[]{:S(2)}) collective-permute-start(bf16[192,1152]{1,0:T(8,128)(2,1)} %bitcast.368), channel_id=1, source_target_pairs={{0,2},{1,3},{2,0},{3,1},{4,6},{5,7},{6,4},{7,5},{8,10},{9,11},{10,... | collective-permute-start | bytes 1327112 | tf_op jit(solution)/shard_map/ppermute | solution.py:135
  47.7 100.7 %collective-permute-start.13 = (bf16[384,1536]{1,0:T(8,128)(2,1)}, bf16[384,1536]{1,0:T(8,128)(2,1)}, u32[]{:S(2)}, u32[]{:S(2)}) collective-permute-start(bf16[384,1536]{1,0:T(8,128)(2,1)} %bitcast.49), channel_id=1, source_target_pairs={{0,2},{1,17},{2,0},{3,19},{4,6},{5,21},{6,4},{7,23},{8,10},{9,25},... | collective-permute-start | bytes 3538952 | tf_op jit(solution)/shard_map/ppermute | solution.py:135
  69.1 286.5 %all-gather.17.cloned.1.call-start = ((), (), s32[]{:S(2)}) async-start(), calls=%async_computation.14 | async-start | bytes 4423680 | tf_op jit(solution)/shard_map/all_gather | solution.py:177
  148.3 5.0 collective-permute-start
  150.4 41.7 %collective-permute-start.14 = (bf16[2,384,1536]{2,1,0:T(8,128)(2,1)S(1)}, bf16[2,384,1536]{2,1,0:T(8,128)(2,1)}, u32[]{:S(2)}, u32[]{:S(2)}) collective-permute-start(bf16[2,384,1536]{2,1,0:T(8,128)(2,1)S(1)} %pad_maximum_fusion.2), channel_id=1, source_target_pairs={{0,16},{1,3},{2,18},{3,1},{4,20},{5,7},{6,22},{7,5},{8,24},{9,11},... | collective-permute-start | bytes 7077896 | tf_op jit(solution)/shard_map/ppermute | solution.py:135
  152.0 13.1 %collective-permute-start.8 = (bf16[192,1152]{1,0:T(8,128)(2,1)S(1)}, bf16[192,1152]{1,0:T(8,128)(2,1)S(1)}, u32[]{:S(2)}, u32[]{:S(2)}) collective-permute-start(bf16[192,1152]{1,0:T(8,128)(2,1)S(1)} %bitcast.403), channel_id=1, source_target_pairs={{0,2},{1,3},{2,0},{3,1},{4,6},{5,7},{6,4},{7,5},{8,10},{9,11},{10,... | collective-permute-start | bytes 1327112 | tf_op jit(solution)/shard_map/ppermute | solution.py:135
  156.8 45.6 %collective-permute-start.1 = (bf16[384,1536]{1,0:T(8,128)(2,1)S(1)}, bf16[384,1536]{1,0:T(8,128)(2,1)S(1)}, u32[]{:S(2)}, u32[]{:S(2)}) collective-permute-start(bf16[384,1536]{1,0:T(8,128)(2,1)S(1)} %get-tuple-element.25), channel_id=1, source_target_pairs={{0,2},{1,17},{2,0},{3,19},{4,6},{5,21},{6,4},{7,23},{8,10},{9,25},... | collective-permute-start | bytes 3538952 | tf_op jit(solution)/shard_map/ppermute | solution.py:135
  158.3 53.0 %collective-permute-start.15 = (bf16[384,1536]{1,0:T(8,128)(2,1)}, bf16[384,1536]{1,0:T(8,128)(2,1)S(1)}, u32[]{:S(2)}, u32[]{:S(2)}) collective-permute-start(bf16[384,1536]{1,0:T(8,128)(2,1)} %bitcast.49), channel_id=1, source_target_pairs={{0,1},{1,0},{2,3},{3,2},{4,5},{5,4},{6,7},{7,6},{8,9},{9,8},{10,11... | collective-permute-start | bytes 3538952 | tf_op jit(solution)/shard_map/ppermute | solution.py:135
  192.0 21.5 %collective-permute-start.17 = (bf16[2,384,1536]{2,1,0:T(8,128)(2,1)}, bf16[2,384,1536]{2,1,0:T(8,128)(2,1)}, u32[]{:S(2)}, u32[]{:S(2)}) collective-permute-start(bf16[2,384,1536]{2,1,0:T(8,128)(2,1)} %collective-permute-done.14), channel_id=1, source_target_pairs={{0,1},{1,0},{2,3},{3,2},{4,5},{5,4},{6,7},{7,6},{8,9},{9,8},{10,11... | collective-permute-start | bytes 7077896 | tf_op jit(solution)/shard_map/ppermute | solution.py:135
  202.3 310.5 %reduce-scatter.14.cloned.1.call-start = ((), (), s32[]{:S(2)}) async-start(), calls=%async_computation.11 | async-start | bytes 4423680 | tf_op jit(solution)/shard_map/reduce_scatter | solution.py:182
  202.3 10.1 %collective-permute-start.16 = (bf16[384,1536]{1,0:T(8,128)(2,1)}, bf16[384,1536]{1,0:T(8,128)(2,1)S(1)}, u32[]{:S(2)}, u32[]{:S(2)}) collective-permute-start(bf16[384,1536]{1,0:T(8,128)(2,1)} %collective-permute-done.13), channel_id=1, source_target_pairs={{0,1},{1,0},{2,3},{3,2},{4,5},{5,4},{6,7},{7,6},{8,9},{9,8},{10,11... | collective-permute-start | bytes 3538952 | tf_op jit(solution)/shard_map/ppermute | solution.py:135
  202.6 28.9 %collective-permute-start.2 = (bf16[2,384,1536]{2,1,0:T(8,128)(2,1)S(1)}, bf16[2,384,1536]{2,1,0:T(8,128)(2,1)S(1)}, u32[]{:S(2)}, u32[]{:S(2)}) collective-permute-start(bf16[2,384,1536]{2,1,0:T(8,128)(2,1)S(1)} %pad_maximum_fusion), channel_id=1, source_target_pairs={{0,16},{1,3},{2,18},{3,1},{4,20},{5,7},{6,22},{7,5},{8,24},{9,11},... | collective-permute-start | bytes 7077896 | tf_op jit(solution)/shard_map/ppermute | solution.py:135
  231.5 9.0 %collective-permute-start.5 = (bf16[2,384,1536]{2,1,0:T(8,128)(2,1)S(1)}, bf16[2,384,1536]{2,1,0:T(8,128)(2,1)S(1)}, u32[]{:S(2)}, u32[]{:S(2)}) collective-permute-start(bf16[2,384,1536]{2,1,0:T(8,128)(2,1)S(1)} %collective-permute-done.2), channel_id=1, source_target_pairs={{0,1},{1,0},{2,3},{3,2},{4,5},{5,4},{6,7},{7,6},{8,9},{9,8},{10,11... | collective-permute-start | bytes 7077896 | tf_op jit(solution)/shard_map/ppermute | solution.py:135
  233.9 3.9 collective-permute-start.3
  234.4 5.0 collective-permute-start.4
  403.3 134.3 %reduce-scatter.12.cloned.1.call-start = ((), (), s32[]{:S(2)}) async-start(), calls=%async_computation.10 | async-start | bytes 4423680 | tf_op jit(solution)/shard_map/reduce_scatter | solution.py:182
  421.4 185.2 %reduce-scatter.10.cloned.1.call-start = ((), (), s32[]{:S(2)}) async-start(), calls=%async_computation.9 | async-start | bytes 4423680 | tf_op jit(solution)/shard_map/reduce_scatter | solution.py:182
  432.3 50.5 %collective-permute-start.9 = (bf16[1536,1536]{1,0:T(8,128)(2,1)}, bf16[1536,1536]{1,0:T(8,128)(2,1)}, u32[]{:S(2)}, u32[]{:S(2)}) collective-permute-start(bf16[1536,1536]{1,0:T(8,128)(2,1)} %convolution_convert_fusion), channel_id=1, source_target_pairs={{0,1},{1,0},{2,3},{3,2},{4,5},{5,4},{6,7},{7,6},{8,9},{9,8},{10,11... | collective-permute-start | bytes 14155784 | tf_op jit(solution)/shard_map/ppermute | solution.py:135
  454.9 39.7 %collective-permute-start.18 = (bf16[1536,1536]{1,0:T(8,128)(2,1)}, bf16[1536,1536]{1,0:T(8,128)(2,1)}, u32[]{:S(2)}, u32[]{:S(2)}) collective-permute-start(bf16[1536,1536]{1,0:T(8,128)(2,1)} %add_convert_fusion), channel_id=1, source_target_pairs={{0,1},{1,0},{2,3},{3,2},{4,5},{5,4},{6,7},{7,6},{8,9},{9,8},{10,11... | collective-permute-start | bytes 14155784 | tf_op jit(solution)/shard_map/ppermute | solution.py:135
  470.0 313.0 %reduce-scatter.8.cloned.1.call-start = ((), (), s32[]{:S(2)}) async-start(), calls=%async_computation.8 | async-start | bytes 2654208 | tf_op jit(solution)/shard_map/reduce_scatter | solution.py:192
  493.2 116.0 %collective-permute-start.10 = (bf16[2,384,1536]{2,1,0:T(8,128)(2,1)}, bf16[2,384,1536]{2,1,0:T(8,128)(2,1)}, u32[]{:S(2)}, u32[]{:S(2)}) collective-permute-start(bf16[2,384,1536]{2,1,0:T(8,128)(2,1)} %bitcast.45), channel_id=1, source_target_pairs={{0,16},{1,3},{2,18},{3,1},{4,20},{5,7},{6,22},{7,5},{8,24},{9,11},... | collective-permute-start | bytes 7077896 | tf_op jit(solution)/shard_map/ppermute | solution.py:135
  508.9 105.0 %collective-permute-start.19 = (bf16[2,384,1536]{2,1,0:T(8,128)(2,1)}, bf16[2,384,1536]{2,1,0:T(8,128)(2,1)}, u32[]{:S(2)}, u32[]{:S(2)}) collective-permute-start(bf16[2,384,1536]{2,1,0:T(8,128)(2,1)} %bitcast.56), channel_id=1, source_target_pairs={{0,16},{1,3},{2,18},{3,1},{4,20},{5,7},{6,22},{7,5},{8,24},{9,11},... | collective-permute-start | bytes 7077896 | tf_op jit(solution)/shard_map/ppermute | solution.py:135
  513.8 104.4 %collective-permute-start.35 = (bf16[192,1152]{1,0:T(8,128)(2,1)S(1)}, bf16[192,1152]{1,0:T(8,128)(2,1)S(1)}, u32[]{:S(2)}, u32[]{:S(2)}) collective-permute-start(bf16[192,1152]{1,0:T(8,128)(2,1)S(1)} %dynamic-slice_bitcast_fusion), channel_id=1, source_target_pairs={{0,2},{1,3},{2,0},{3,1},{4,6},{5,7},{6,4},{7,5},{8,10},{9,11},{10,... | collective-permute-start | bytes 1327112 | tf_op jit(solution)/shard_map/ppermute | solution.py:135
  538.6 81.3 %collective-permute-start.33 = (bf16[192,1152]{1,0:T(8,128)(2,1)S(1)}, bf16[192,1152]{1,0:T(8,128)(2,1)S(1)}, u32[]{:S(2)}, u32[]{:S(2)}) collective-permute-start(bf16[192,1152]{1,0:T(8,128)(2,1)S(1)} %dynamic-slice_bitcast_fusion.1), channel_id=1, source_target_pairs={{0,2},{1,3},{2,0},{3,1},{4,6},{5,7},{6,4},{7,5},{8,10},{9,11},{10,... | collective-permute-start | bytes 1327112 | tf_op jit(solution)/shard_map/ppermute | solution.py:135
  607.6 13.1 %collective-permute-start.31 = (bf16[192,1152]{1,0:T(8,128)(2,1)S(1)}, bf16[192,1152]{1,0:T(8,128)(2,1)S(1)}, u32[]{:S(2)}, u32[]{:S(2)}) collective-permute-start(bf16[192,1152]{1,0:T(8,128)(2,1)S(1)} %dynamic-slice_bitcast_fusion.2), channel_id=1, source_target_pairs={{0,2},{1,3},{2,0},{3,1},{4,6},{5,7},{6,4},{7,5},{8,10},{9,11},{10,... | collective-permute-start | bytes 1327112 | tf_op jit(solution)/shard_map/ppermute | solution.py:135
  613.4 31.9 %collective-permute-start.11 = (bf16[384,1536]{1,0:T(8,128)(2,1)S(1)}, bf16[384,1536]{1,0:T(8,128)(2,1)S(1)}, u32[]{:S(2)}, u32[]{:S(2)}) collective-permute-start(bf16[384,1536]{1,0:T(8,128)(2,1)S(1)} %fusion.54), channel_id=1, source_target_pairs={{0,2},{1,17},{2,0},{3,19},{4,6},{5,21},{6,4},{7,23},{8,10},{9,25},... | collective-permute-start | bytes 3538952 | tf_op jit(solution)/shard_map/ppermute | solution.py:135
  616.6 27.9 %collective-permute-start.20 = (bf16[384,1536]{1,0:T(8,128)(2,1)S(1)}, bf16[384,1536]{1,0:T(8,128)(2,1)S(1)}, u32[]{:S(2)}, u32[]{:S(2)}) collective-permute-start(bf16[384,1536]{1,0:T(8,128)(2,1)S(1)} %fusion.55), channel_id=1, source_target_pairs={{0,2},{1,17},{2,0},{3,19},{4,6},{5,21},{6,4},{7,23},{8,10},{9,25},... | collective-permute-start | bytes 3538952 | tf_op jit(solution)/shard_map/ppermute | solution.py:135
  618.4 44.9 %collective-permute-start.36 = (bf16[2,192,1152]{2,1,0:T(8,128)(2,1)S(1)}, bf16[2,192,1152]{2,1,0:T(8,128)(2,1)}, u32[]{:S(2)}, u32[]{:S(2)}) collective-permute-start(bf16[2,192,1152]{2,1,0:T(8,128)(2,1)S(1)} %pad_maximum_fusion.23), channel_id=1, source_target_pairs={{0,16},{1,17},{2,18},{3,19},{4,20},{5,21},{6,22},{7,23},{8,24},{9,... | collective-permute-start | bytes 2654216 | tf_op jit(solution)/shard_map/ppermute | solution.py:135
  620.1 44.6 %collective-permute-start.34 = (bf16[2,192,1152]{2,1,0:T(8,128)(2,1)S(1)}, bf16[2,192,1152]{2,1,0:T(8,128)(2,1)}, u32[]{:S(2)}, u32[]{:S(2)}) collective-permute-start(bf16[2,192,1152]{2,1,0:T(8,128)(2,1)S(1)} %pad_maximum_fusion.22), channel_id=1, source_target_pairs={{0,16},{1,17},{2,18},{3,19},{4,20},{5,21},{6,22},{7,23},{8,24},{9,... | collective-permute-start | bytes 2654216 | tf_op jit(solution)/shard_map/ppermute | solution.py:135
  620.9 58.0 %collective-permute-start.32 = (bf16[2,192,1152]{2,1,0:T(8,128)(2,1)S(1)}, bf16[2,192,1152]{2,1,0:T(8,128)(2,1)S(1)}, u32[]{:S(2)}, u32[]{:S(2)}) collective-permute-start(bf16[2,192,1152]{2,1,0:T(8,128)(2,1)S(1)} %pad_maximum_fusion.21), channel_id=1, source_target_pairs={{0,16},{1,17},{2,18},{3,19},{4,20},{5,21},{6,22},{7,23},{8,24},{9,... | collective-permute-start | bytes 2654216 | tf_op jit(solution)/shard_map/ppermute | solution.py:135
  648.6 32.6 %collective-permute-start.21 = (bf16[384,1536]{1,0:T(8,128)(2,1)S(1)}, bf16[384,1536]{1,0:T(8,128)(2,1)S(1)}, u32[]{:S(2)}, u32[]{:S(2)}) collective-permute-start(bf16[384,1536]{1,0:T(8,128)(2,1)S(1)} %get-tuple-element.20), channel_id=1, source_target_pairs={{0,1},{1,0},{2,3},{3,2},{4,5},{5,4},{6,7},{7,6},{8,9},{9,8},{10,11... | collective-permute-start | bytes 3538952 | tf_op jit(solution)/shard_map/ppermute | solution.py:135
  663.2 102.0 %collective-permute-start.12 = (bf16[384,1536]{1,0:T(8,128)(2,1)}, bf16[384,1536]{1,0:T(8,128)(2,1)}, u32[]{:S(2)}, u32[]{:S(2)}) collective-permute-start(bf16[384,1536]{1,0:T(8,128)(2,1)} %get-tuple-element.37), channel_id=1, source_target_pairs={{0,1},{1,0},{2,3},{3,2},{4,5},{5,4},{6,7},{7,6},{8,9},{9,8},{10,11... | collective-permute-start | bytes 3538952 | tf_op jit(solution)/shard_map/ppermute | solution.py:135
  686.4 164.7 %reduce-scatter.6.cloned.1.call-start = ((), (), s32[]{:S(2)}) async-start(), calls=%async_computation.7 | async-start | bytes 3538944 | tf_op jit(solution)/shard_map/reduce_scatter | solution.py:192
  741.9 20.9 %collective-permute-start.22 = (bf16[384,1536]{1,0:T(8,128)(2,1)S(1)}, bf16[384,1536]{1,0:T(8,128)(2,1)S(1)}, u32[]{:S(2)}, u32[]{:S(2)}) collective-permute-start(bf16[384,1536]{1,0:T(8,128)(2,1)S(1)} %fusion.53), channel_id=1, source_target_pairs={{0,1},{1,0},{2,3},{3,2},{4,5},{5,4},{6,7},{7,6},{8,9},{9,8},{10,11... | collective-permute-start | bytes 3538952 | tf_op jit(solution)/shard_map/ppermute | solution.py:135
  763.6 3.8 collective-permute-start.24
  767.4 3.7 collective-permute-start.25
  771.2 3.8 collective-permute-start.26
  774.5 7.0 collective-permute-start.23
  775.0 4.7 collective-permute-start.27
  779.8 1.2 collective-permute-start.28
  783.0 71.2 %copy-start.38 = (bf16[192,768]{1,0:T(8,128)(2,1)S(1)}, bf16[192,768]{1,0:T(8,128)(2,1)}, u32[]{:S(2)}) copy-start(bf16[192,768]{1,0:T(8,128)(2,1)} %reduce-scatter.8.cloned.1.call-done) | copy-start | bytes 884740
  783.0 71.1 %collective-permute-start.30 = (bf16[192,768]{1,0:T(8,128)(2,1)}, bf16[192,768]{1,0:T(8,128)(2,1)S(1)}, u32[]{:S(2)}, u32[]{:S(2)}) collective-permute-start(bf16[192,768]{1,0:T(8,128)(2,1)} %reduce-scatter.8.cloned.1.call-done), channel_id=1, source_target_pairs={{0,16},{1,17},{2,18},{3,19},{4,20},{5,21},{6,22},{7,23},{8,24},{9,... | collective-permute-start | bytes 884744 | tf_op jit(solution)/shard_map/ppermute | solution.py:135
  851.1 10.4 %collective-permute-start.29 = (bf16[192,1024]{1,0:T(8,128)(2,1)}, bf16[192,1024]{1,0:T(8,128)(2,1)S(1)}, u32[]{:S(2)}, u32[]{:S(2)}) collective-permute-start(bf16[192,1024]{1,0:T(8,128)(2,1)} %reduce-scatter.6.cloned.1.call-done), channel_id=1, source_target_pairs={{0,16},{1,17},{2,18},{3,19},{4,20},{5,21},{6,22},{7,23},{8,24},{9,... | collective-permute-start | bytes 1179656 | tf_op jit(solution)/shard_map/ppermute | solution.py:135
  (73 other events, 724.7 us)
Sparse Core Ops, SparseCore 0:
  10.7 80.7 all-gather.8
  93.7 50.6 all-gather.10
  146.0 68.4 all-gather.14
  216.5 68.5 all-gather.12
  287.0 68.5 all-gather.16
  403.4 65.0 reduce-scatter.13
  470.8 66.6 reduce-scatter.11
  539.8 66.6 reduce-scatter.9
  686.5 87.1 reduce-scatter.7
  777.1 73.9 reduce-scatter.5
where the time goes:
time: 877 us; the launch traced here: 870 us
  waiting for transfers between devices  384 us (44%)
  matrix products  240 us (27%)
  local copies, waits for them, and re-layouts  87.7 us (10%)
  starting transfers between devices  76.5 us (9%)
  other arithmetic  66.3 us (8%)
  between operations  15.9 us (2%)
    ppermute x34, waiting for transfers between devices, send(): return lax.ppermute(value, AXES, table[route])  114 us
    reduce_scatter x3, waiting for transfers between devices, ffn_scatter(): lax.psum_scatter(parts, 'dp', scatter_dimension=0, axis_index_groups=line...  88.7 us
    all_gather x3, waiting for transfers between devices, ffn_gather(): full = lax.all_gather(pair, 'dp', axis=0, axis_index_groups=line_groups)  77.1 us
    dot_general x8, matrix products, trans_dot(): lax.dot_general(left_side, right_side, (((1,), (1,)), ((), ())), preferre...  75.4 us
    dot_general x5, matrix products, plain_dot(): return jnp.dot(left_side, right_side, preferred_element_type=jnp.float32)  74.3 us
    ppermute x34, starting transfers between devices, send(): return lax.ppermute(value, AXES, table[route])  70.9 us
    reduce_scatter x2, waiting for transfers between devices, attn_scatter(): lax.psum_scatter(grad.astype(bf16), 'dp', scatter_dimension=0, tiled=True)  66.6 us
    dot_general x5, matrix products, outer_dot(): lax.dot_general(left_side, right_side, (((0,), (0,)), ((), ())), preferre...  59.6 us
  transfers between devices with their start and end apart: 47, of which 21 were waited for; matrix products, arithmetic and copies ran while one was open for 38% of the time, Pallas kernels for 0%

commit v1 on v0

--- a/solution.py
+++ b/solution.py
@@ -203,9 +203,24 @@
     query_cols = head_count * HD
     key_cols = kv_count * HD
     qkv_cols = query_cols + 2 * key_cols
-    qkv_full = lax.all_gather(
-        jnp.concatenate([w_query, w_key, w_value, gains], axis=1), "dp", axis=0, tiled=True
-    )
+    array = jnp.concatenate([w_query, w_key, w_value, gains], axis=1)
+    length, place, span = (lax.axis_size("dp"), lax.axis_index("dp"), array.shape[0])
+    right = [(i_2, (i_2 + 1) % length) for i_2 in range(length)]
+    downward = [(i_2, (i_2 - 1) % length) for i_2 in range(length)]
+    qkv_full = jnp.zeros((*array.shape[:0], length * span, *array.shape[0 + 1 :]), array.dtype)
+    qkv_full = lax.dynamic_update_slice_in_dim(qkv_full, array, place * span, axis=0)
+    from_left = from_right = array
+    halfway = length // 2
+    for k in range(1, halfway + 1):
+        from_left = lax.ppermute(from_left, "dp", right)
+        qkv_full = lax.dynamic_update_slice_in_dim(
+            qkv_full, from_left, (place - k) % length * span, axis=0
+        )
+        if k < length - halfway:
+            from_right = lax.ppermute(from_right, "dp", downward)
+            qkv_full = lax.dynamic_update_slice_in_dim(
+                qkv_full, from_right, (place + k) % length * span, axis=0
+            )
     out_full = lax.all_gather(w_out, "dp", axis=0, tiled=True)
     gate_full = ffn_gather(w_gate)
     up_full = ffn_gather(w_up)

time: 877 us -> 922 us (1.051)
  local copies, waits for them, and re-layouts: 87.7 us -> 153 us
  waiting for transfers between devices: 384 us -> 343 us
  starting transfers between devices: 76.5 us -> 94.4 us
    all_gather x3, waiting for transfers between devices: 77.1 us -> 6.92 us  [ffn_gather(): full = lax.all_gather(pair, 'dp', axis=0, axis_index_groups=line_groups)]
    ppermute x0 -> x7, waiting for transfers between devices: none -> 68.3 us  [the longest x4 68.3 us: local(): from_left = lax.ppermute(from_left, 'dp', right)]
    dynamic_update_slice x0 -> x8, local copies, waits for them, and re-layouts: none -> 56.3 us  [the longest x4 27.7 us: local(): lax.dynamic_update_slice_in_dim(qkv_full, from_left, (place - k) % length...]
    all_gather x1 -> x0, waiting for transfers between devices: 22.2 us -> none  [local(): lax.all_gather(jnp.concatenate([w_query, w_key, w_value, gains], axis=1),...]
    ppermute x0 -> x7, starting transfers between devices: none -> 18.3 us  [the longest x3 13.4 us: local(): from_right = lax.ppermute(from_right, 'dp', downward)]
    ppermute x34, waiting for transfers between devices: 114 us -> 100 us  [send(): return lax.ppermute(value, AXES, table[route])]
    all_gather x1, waiting for transfers between devices: 10.9 us -> 0.02 us  [local(): out_full = lax.all_gather(w_out, 'dp', axis=0, tiled=True)]
    unnamed x164 -> x180, local copies, waits for them, and re-layouts: 37.1 us -> 36.6 us
  transfers between devices with their start and end apart: 47 -> 53, of which waited for: 21 -> 19; matrix products, arithmetic and copies ran while one was open for 38% -> 43% of each run, Pallas kernels for 0% -> 0%
where the time goes in v1:
time: 922 us; the launch traced here: 912 us
  waiting for transfers between devices  343 us (37%)
  matrix products  242 us (26%)
  local copies, waits for them, and re-layouts  153 us (17%)
  starting transfers between devices  94.4 us (10%)
  other arithmetic  64.3 us (7%)
  between operations  15.5 us (2%)
    ppermute x34, waiting for transfers between devices, send(): return lax.ppermute(value, AXES, table[route])  100 us
    reduce_scatter x3, waiting for transfers between devices, ffn_scatter(): lax.psum_scatter(parts, 'dp', scatter_dimension=0, axis_index_groups=line...  95.8 us
    dot_general x8, matrix products, trans_dot(): lax.dot_general(left_side, right_side, (((1,), (1,)), ((), ())), preferre...  75.9 us
    dot_general x5, matrix products, plain_dot(): return jnp.dot(left_side, right_side, preferred_element_type=jnp.float32)  74.6 us
    ppermute x34, starting transfers between devices, send(): return lax.ppermute(value, AXES, table[route])  70.2 us
    ppermute x4, waiting for transfers between devices, local(): from_left = lax.ppermute(from_left, 'dp', right)  68.3 us
    reduce_scatter x2, waiting for transfers between devices, attn_scatter(): lax.psum_scatter(grad.astype(bf16), 'dp', scatter_dimension=0, tiled=True)  67.1 us
    dot_general x5, matrix products, outer_dot(): lax.dot_general(left_side, right_side, (((0,), (0,)), ((), ())), preferre...  59.6 us
  transfers between devices with their start and end apart: 53, of which 19 were waited for; matrix products, arithmetic and copies ran while one was open for 43% of the time, Pallas kernels for 0%

profile of v1, /device:TPU:0, one launch (start us, length us, event | category | flops | bytes accessed | tf_op | source)
XLA Modules:
  0.0 911.9 jit_solution(15033477507843995306)
XLA Ops:
  13.6 6.5 constant_dynamic-slice_fusion.4
  23.3 12.9 %collective-permute-done.14 = bf16[192,1152]{1,0:T(8,128)(2,1)S(1)} collective-permute-done((bf16[192,1152]{1,0:T(8,128)(2,1)S(1)}, bf16[192,1152]{1,0:T(8,128)(2,1)S(1)}, u32[]{:S(2)}, u32[]{:S(2)}) %collective-permute-start.14) | collective-permute-done | bytes 442400 | tf_op jit(solution)/shard_map/ppermute | solution.py:135
  55.9 6.9 dynamic_update_slice.24
  63.0 5.5 collective-permute-done
  72.5 4.5 collective-permute-start.3
  77.0 47.3 %collective-permute-done.2 = bf16[192,1152]{1,0:T(8,128)(2,1)S(1)} collective-permute-done((bf16[192,1152]{1,0:T(8,128)(2,1)}, bf16[192,1152]{1,0:T(8,128)(2,1)S(1)}, u32[]{:S(2)}, u32[]{:S(2)}) %collective-permute-start.2) | collective-permute-done | bytes 442400 | tf_op jit(solution)/shard_map/ppermute | solution.py:215
  127.9 5.6 collective-permute-start.5
  133.5 15.6 %collective-permute-done.4 = bf16[192,1152]{1,0:T(8,128)(2,1)} collective-permute-done((bf16[192,1152]{1,0:T(8,128)(2,1)S(1)}, bf16[192,1152]{1,0:T(8,128)(2,1)}, u32[]{:S(2)}, u32[]{:S(2)}) %collective-permute-start.4) | collective-permute-done | bytes 442400 | tf_op jit(solution)/shard_map/ppermute | solution.py:215
  153.0 6.8 dynamic_update_slice.25
  161.1 7.5 dynamic_update_slice.26
  168.8 6.5 dynamic_update_slice.27
  176.6 6.7 dynamic_update_slice.28
  184.6 7.6 dynamic_update_slice.29
  193.4 7.5 dynamic_update_slice.30
  202.2 6.8 dynamic_update_slice.31
  209.8 4.5 fusion.41
  242.4 4.7 fusion.44
  264.0 6.8 collective-permute-done.15
  270.9 26.7 %collective-permute-done.21 = bf16[2,384,1536]{2,1,0:T(8,128)(2,1)} collective-permute-done((bf16[2,384,1536]{2,1,0:T(8,128)(2,1)S(1)}, bf16[2,384,1536]{2,1,0:T(8,128)(2,1)}, u32[]{:S(2)}, u32[]{:S(2)}) %collective-permute-start.21) | collective-permute-done | bytes 2359328 | tf_op jit(solution)/shard_map/ppermute | solution.py:135
  297.6 8.8 collective-permute-start.24
  321.1 15.6 %collective-permute-done.9 = bf16[2,384,1536]{2,1,0:T(8,128)(2,1)S(1)} collective-permute-done((bf16[2,384,1536]{2,1,0:T(8,128)(2,1)S(1)}, bf16[2,384,1536]{2,1,0:T(8,128)(2,1)S(1)}, u32[]{:S(2)}, u32[]{:S(2)}) %collective-permute-start.9) | collective-permute-done | bytes 2359328 | tf_op jit(solution)/shard_map/ppermute | solution.py:135
  347.4 18.1 %fusion.108 = f32[3072,1152]{1,0:T(8,128)} fusion(bf16[3072,1536]{1,0:T(8,128)(2,1)} %fusion.60, bf16[1536,1152]{1,0:T(8,128)(2,1)} %bitcast.411), kind=kOutput, calls=%fused_computation.273 | convolution fusion | flops 10871635968 | bytes 27131904 | tf_op jit(solution)/shard_map/dot_general | solution.py:54
  365.5 17.9 %fusion.107 = f32[3072,1152]{1,0:T(8,128)} fusion(bf16[3072,1536]{1,0:T(8,128)(2,1)} %fusion.60, bf16[1536,1152]{1,0:T(8,128)(2,1)} %bitcast.414), kind=kOutput, calls=%fused_computation.272 | convolution fusion | flops 10871635968 | bytes 27131904 | tf_op jit(solution)/shard_map/dot_general | solution.py:54
  383.4 6.9 all-gather.14.cloned.1.call-done
  390.3 29.6 %multiply_convert_fusion = (bf16[3072,1152]{1,0:T(8,128)(2,1)}, bf16[3072,1152]{1,0:T(8,128)(2,1)}, bf16[3072,1152]{1,0:T(8,128)(2,1)}) fusion(f32[3072,1152]{1,0:T(8,128)} %fusion.107, f32[3072,1152]{1,0:T(8,128)} %fusion.108, bf16[3072,1536]{1,0:T(8,128)(2,1)} %fusion.56, bf16[1536,1152]{1,0:T(8,128)(2,1)} %bitcast.417), kind=kOutput, calls=%fused_computation.7 | convolution fusion | flops 10924720128 | bytes 62521344 | tf_op jit(solution)/shard_map/dot_general | solution.py:54
  420.0 18.2 %convolution_convert_fusion.1 = bf16[1536,1152]{1,0:T(8,128)(2,1)} fusion(bf16[3072,1536]{1,0:T(8,128)(2,1)} %fusion.56, bf16[3072,1152]{1,0:T(8,128)(2,1)} %get-tuple-element.30), kind=kOutput, calls=%fused_computation.20 | convolution fusion | flops 10873405440 | bytes 20054016 | tf_op jit(solution)/shard_map/dot_general | solution.py:64
  438.2 18.0 %convolution_convert_fusion.2 = bf16[1536,1152]{1,0:T(8,128)(2,1)} fusion(bf16[3072,1536]{1,0:T(8,128)(2,1)} %fusion.60, bf16[3072,1152]{1,0:T(8,128)(2,1)} %get-tuple-element.28), kind=kOutput, calls=%fused_computation.21 | convolution fusion | flops 10873405440 | bytes 20054016 | tf_op jit(solution)/shard_map/dot_general | solution.py:64
  456.2 11.4 %convolution_convert_fusion = bf16[1536,1536]{1,0:T(8,128)(2,1)} fusion(bf16[1536,1152]{1,0:T(8,128)(2,1)} %bitcast.418, bf16[3072,1152]{1,0:T(8,128)(2,1)} %get-tuple-element.30), kind=kOutput, calls=%fused_computation.19 | convolution fusion | flops 5438177280 | bytes 11796480 | tf_op jit(solution)/shard_map/dot_general | solution.py:58
  467.6 11.0 %fusion.14 = f32[1536,1536]{1,0:T(8,128)} fusion(bf16[1536,1152]{1,0:T(8,128)(2,1)S(1)} %bitcast.415, bf16[3072,1152]{1,0:T(8,128)(2,1)} %get-tuple-element.29), kind=kOutput, calls=%fused_computation.37 | convolution fusion | flops 5435817984 | bytes 16515072 | tf_op jit(solution)/shard_map/dot_general | solution.py:58
  478.7 11.7 %add_convert_fusion = bf16[1536,1536]{1,0:T(8,128)(2,1)} fusion(f32[1536,1536]{1,0:T(8,128)} %fusion.14, bf16[1536,1152]{1,0:T(8,128)(2,1)S(1)} %bitcast.413, bf16[3072,1152]{1,0:T(8,128)(2,1)} %get-tuple-element.28), kind=kOutput, calls=%fused_computation.17 | convolution fusion | flops 5440536576 | bytes 21233664 | tf_op jit(solution)/shard_map/dot_general | solution.py:58
  490.8 14.5 %convolution_convert_fusion.3 = bf16[1536,1152]{1,0:T(8,128)(2,1)} fusion(bf16[3072,1536]{1,0:T(8,128)(2,1)S(1)} %bitcast.406, bf16[3072,1152]{1,0:T(8,128)(2,1)S(1)} %bitcast.422), kind=kOutput, calls=%fused_computation.22 | convolution fusion | flops 10873405440 | bytes 20054016 | tf_op jit(solution)/shard_map/dot_general | solution.py:64
  506.1 11.2 %fusion.17 = f32[1536,1536]{1,0:T(8,128)} fusion(bf16[1536,1152]{1,0:T(8,128)(2,1)S(1)} %bitcast.416, bf16[3072,1152]{1,0:T(8,128)(2,1)} %get-tuple-element.29), kind=kOutput, calls=%fused_computation.40 | convolution fusion | flops 5435817984 | bytes 16515072 | tf_op jit(solution)/shard_map/dot_general | solution.py:58
  517.3 9.2 %convert_add_fusion.1 = f32[1536,1536]{1,0:T(8,128)S(1)} fusion(bf16[1536,1536]{1,0:T(8,128)(2,1)} %collective-permute-done.16, bf16[1536,1152]{1,0:T(8,128)(2,1)S(1)} %bitcast.419, bf16[3072,1152]{1,0:T(8,128)(2,1)} %get-tuple-element.30), kind=kOutput, calls=%fused_computation.18 | convolution fusion | flops 5440536576 | bytes 21233664 | tf_op jit(solution)/shard_map/dot_general | solution.py:58
  529.4 12.5 %convert_add_fusion = f32[1536,1536]{1,0:T(8,128)S(1)} fusion(bf16[1536,1536]{1,0:T(8,128)(2,1)} %collective-permute-done.25, f32[1536,1536]{1,0:T(8,128)} %fusion.17, bf16[1536,1152]{1,0:T(8,128)(2,1)} %bitcast.412, bf16[3072,1152]{1,0:T(8,128)(2,1)} %get-tuple-element.28), kind=kOutput, calls=%fused_computation.16 | convolution fusion | flops 5442895872 | bytes 30670848 | tf_op jit(solution)/shard_map/dot_general | solution.py:58
  550.2 29.3 %reduce-scatter.12.cloned.1.call-done = bf16[1,384,1152]{2,1,0:T(8,128)(2,1)} async-done(((bf16[4,384,1152]{2,1,0:T(8,128)(2,1)}), bf16[1,384,1152]{2,1,0:T(8,128)(2,1)}) %reduce-scatter.12.cloned.1.call-update) | async-done | bytes 884752 | tf_op jit(solution)/shard_map/reduce_scatter | solution.py:182
  582.1 66.5 %reduce-scatter.10.cloned.1.call-done = bf16[1,384,1152]{2,1,0:T(8,128)(2,1)} async-done(((bf16[4,384,1152]{2,1,0:T(8,128)(2,1)}), bf16[1,384,1152]{2,1,0:T(8,128)(2,1)}) %reduce-scatter.10.cloned.1.call-update) | async-done | bytes 884752 | tf_op jit(solution)/shard_map/reduce_scatter | solution.py:182
  664.4 22.0 %collective-permute-done.27 = bf16[384,1536]{1,0:T(8,128)(2,1)S(1)} collective-permute-done((bf16[384,1536]{1,0:T(8,128)(2,1)S(1)}, bf16[384,1536]{1,0:T(8,128)(2,1)S(1)}, u32[]{:S(2)}, u32[]{:S(2)}) %collective-permute-start.27) | collective-permute-done | bytes 1179680 | tf_op jit(solution)/shard_map/ppermute | solution.py:135
  690.6 14.7 %collective-permute-start.28 = (bf16[384,1536]{1,0:T(8,128)(2,1)S(1)}, bf16[384,1536]{1,0:T(8,128)(2,1)S(1)}, u32[]{:S(2)}, u32[]{:S(2)}) collective-permute-start(bf16[384,1536]{1,0:T(8,128)(2,1)S(1)} %get-tuple-element.20), channel_id=1, source_target_pairs={{0,1},{1,0},{2,3},{3,2},{4,5},{5,4},{6,7},{7,6},{8,9},{9,8},{10,11... | collective-permute-start | bytes 3538952 | tf_op jit(solution)/shard_map/ppermute | solution.py:135
  712.0 8.8 collective-permute-done.39
  728.4 4.4 convolution_convert_fusion.6
  732.9 12.4 %fusion = (f32[6,768]{1,0:T(8,128)S(1)}, f32[768,768,6]{1,0,2:T(8,128)}) fusion(f32[1,6,768,768]{2,3,1,0:T(8,128)} %copy-done, f32[6,768]{1,0:T(8,128)S(1)} %log_add_fusion, bf16[768,6,128]{0,2,1:T(8,128)(2,1)S(1)} %bitcast.387, f32[768,1024]{1,0:T(8,128)} %copy-done.10), kind=kOutput, calls=%fused_computation.3 | convolution fusion | flops 916581888 | bytes 29724672 | tf_op jit(solution)/shard_map/qkgd,skd->kgqs/dot_general | solution.py:292
  747.4 7.8 fusion.9
  761.9 4.4 bitcast_multiply_fusion.1
  772.3 5.5 convolution_convert_fusion.4
  777.8 5.2 fusion.24
  783.2 18.5 %collective-permute-start.29 = (bf16[384,1536]{1,0:T(8,128)(2,1)S(1)}, bf16[384,1536]{1,0:T(8,128)(2,1)S(1)}, u32[]{:S(2)}, u32[]{:S(2)}) collective-permute-start(bf16[384,1536]{1,0:T(8,128)(2,1)S(1)} %fusion.53), channel_id=1, source_target_pairs={{0,1},{1,0},{2,3},{3,2},{4,5},{5,4},{6,7},{7,6},{8,9},{9,8},{10,11... | collective-permute-start | bytes 3538952 | tf_op jit(solution)/shard_map/ppermute | solution.py:135
  826.0 67.1 %reduce-scatter.6.cloned.1.call-done = bf16[192,1024]{1,0:T(8,128)(2,1)} async-done(((bf16[1536,1024]{1,0:T(8,128)(2,1)}), bf16[192,1024]{1,0:T(8,128)(2,1)}) %reduce-scatter.6.cloned.1.call-update) | async-done | bytes 393232 | tf_op jit(solution)/shard_map/reduce_scatter | solution.py:192
  897.1 6.5 collective-permute-done.36
  (417 shorter events, 211.8 us)
Async XLA Ops:
  7.2 242.8 %all-gather.8.cloned.1.call-start = ((), (), s32[]{:S(2)}) async-start(), calls=%async_computation.5 | async-start | bytes 2654208 | tf_op jit(solution)/shard_map/all_gather | solution.py:224
  7.9 339.5 %all-gather.12.cloned.1.call-start = ((), (), s32[]{:S(2)}) async-start(), calls=%async_computation.12 | async-start | bytes 4423680 | tf_op jit(solution)/shard_map/all_gather | solution.py:177
  20.2 16.0 %collective-permute-start.14 = (bf16[192,1152]{1,0:T(8,128)(2,1)S(1)}, bf16[192,1152]{1,0:T(8,128)(2,1)S(1)}, u32[]{:S(2)}, u32[]{:S(2)}) collective-permute-start(bf16[192,1152]{1,0:T(8,128)(2,1)S(1)} %bitcast.404), channel_id=1, source_target_pairs={{0,2},{1,3},{2,0},{3,1},{4,6},{5,7},{6,4},{7,5},{8,10},{9,11},{10,... | collective-permute-start | bytes 1327112 | tf_op jit(solution)/shard_map/ppermute | solution.py:135
  37.4 328.1 %all-gather.10.cloned.1.call-start = ((), (), s32[]{:S(2)}) async-start(), calls=%async_computation.11 | async-start | bytes 4423680 | tf_op jit(solution)/shard_map/all_gather | solution.py:177
  38.5 34.0 %collective-permute-start.1 = (bf16[192,1152]{1,0:T(8,128)(2,1)}, bf16[192,1152]{1,0:T(8,128)(2,1)}, u32[]{:S(2)}, u32[]{:S(2)}) collective-permute-start(bf16[192,1152]{1,0:T(8,128)(2,1)} %fusion.73), channel_id=1, source_target_pairs={{0,14},{2,0},{4,2},{6,4},{8,6},{10,8},{12,10},{14,12},{1,15},{3,1}... | collective-permute-start | bytes 1327112 | tf_op jit(solution)/shard_map/ppermute | solution.py:220
  41.8 26.6 %collective-permute-start = (bf16[192,1152]{1,0:T(8,128)(2,1)}, bf16[192,1152]{1,0:T(8,128)(2,1)}, u32[]{:S(2)}, u32[]{:S(2)}) collective-permute-start(bf16[192,1152]{1,0:T(8,128)(2,1)} %fusion.73), channel_id=1, source_target_pairs={{0,2},{2,4},{4,6},{6,8},{8,10},{10,12},{12,14},{14,0},{1,3},{3,5},... | collective-permute-start | bytes 1327112 | tf_op jit(solution)/shard_map/ppermute | solution.py:215
  46.6 102.5 %collective-permute-start.13 = (bf16[192,1152]{1,0:T(8,128)(2,1)}, bf16[192,1152]{1,0:T(8,128)(2,1)}, u32[]{:S(2)}, u32[]{:S(2)}) collective-permute-start(bf16[192,1152]{1,0:T(8,128)(2,1)} %bitcast.368), channel_id=1, source_target_pairs={{0,2},{1,3},{2,0},{3,1},{4,6},{5,7},{6,4},{7,5},{8,10},{9,11},{10,... | collective-permute-start | bytes 1327112 | tf_op jit(solution)/shard_map/ppermute | solution.py:135
  49.5 204.5 %collective-permute-start.20 = (bf16[384,1536]{1,0:T(8,128)(2,1)}, bf16[384,1536]{1,0:T(8,128)(2,1)}, u32[]{:S(2)}, u32[]{:S(2)}) collective-permute-start(bf16[384,1536]{1,0:T(8,128)(2,1)} %bitcast.49), channel_id=1, source_target_pairs={{0,2},{1,17},{2,0},{3,19},{4,6},{5,21},{6,4},{7,23},{8,10},{9,25},... | collective-permute-start | bytes 3538952 | tf_op jit(solution)/shard_map/ppermute | solution.py:135
  68.5 55.9 %collective-permute-start.2 = (bf16[192,1152]{1,0:T(8,128)(2,1)}, bf16[192,1152]{1,0:T(8,128)(2,1)S(1)}, u32[]{:S(2)}, u32[]{:S(2)}) collective-permute-start(bf16[192,1152]{1,0:T(8,128)(2,1)} %collective-permute-done), channel_id=1, source_target_pairs={{0,2},{2,4},{4,6},{6,8},{8,10},{10,12},{12,14},{14,0},{1,3},{3,5},... | collective-permute-start | bytes 1327112 | tf_op jit(solution)/shard_map/ppermute | solution.py:215
  72.5 55.4 %collective-permute-start.3 = (bf16[192,1152]{1,0:T(8,128)(2,1)}, bf16[192,1152]{1,0:T(8,128)(2,1)}, u32[]{:S(2)}, u32[]{:S(2)}) collective-permute-start(bf16[192,1152]{1,0:T(8,128)(2,1)} %collective-permute-done.1), channel_id=1, source_target_pairs={{0,14},{2,0},{4,2},{6,4},{8,6},{10,8},{12,10},{14,12},{1,15},{3,1}... | collective-permute-start | bytes 1327112 | tf_op jit(solution)/shard_map/ppermute | solution.py:220
  124.3 24.7 %collective-permute-start.4 = (bf16[192,1152]{1,0:T(8,128)(2,1)S(1)}, bf16[192,1152]{1,0:T(8,128)(2,1)}, u32[]{:S(2)}, u32[]{:S(2)}) collective-permute-start(bf16[192,1152]{1,0:T(8,128)(2,1)S(1)} %collective-permute-done.2), channel_id=1, source_target_pairs={{0,2},{2,4},{4,6},{6,8},{8,10},{10,12},{12,14},{14,0},{1,3},{3,5},... | collective-permute-start | bytes 1327112 | tf_op jit(solution)/shard_map/ppermute | solution.py:215
  127.9 64.3 %collective-permute-start.5 = (bf16[192,1152]{1,0:T(8,128)(2,1)}, bf16[192,1152]{1,0:T(8,128)(2,1)}, u32[]{:S(2)}, u32[]{:S(2)}) collective-permute-start(bf16[192,1152]{1,0:T(8,128)(2,1)} %collective-permute-done.3), channel_id=1, source_target_pairs={{0,14},{2,0},{4,2},{6,4},{8,6},{10,8},{12,10},{14,12},{1,15},{3,1}... | collective-permute-start | bytes 1327112 | tf_op jit(solution)/shard_map/ppermute | solution.py:220
  149.1 51.9 %collective-permute-start.6 = (bf16[192,1152]{1,0:T(8,128)(2,1)}, bf16[192,1152]{1,0:T(8,128)(2,1)}, u32[]{:S(2)}, u32[]{:S(2)}) collective-permute-start(bf16[192,1152]{1,0:T(8,128)(2,1)} %collective-permute-done.4), channel_id=1, source_target_pairs={{0,2},{2,4},{4,6},{6,8},{8,10},{10,12},{12,14},{14,0},{1,3},{3,5},... | collective-permute-start | bytes 1327112 | tf_op jit(solution)/shard_map/ppermute | solution.py:215
  151.3 239.1 %all-gather.14.cloned.1.call-start = ((), (), s32[]{:S(2)}) async-start(), calls=%async_computation.13 | async-start | bytes 4423680 | tf_op jit(solution)/shard_map/all_gather | solution.py:177
  256.0 41.7 %collective-permute-start.21 = (bf16[2,384,1536]{2,1,0:T(8,128)(2,1)S(1)}, bf16[2,384,1536]{2,1,0:T(8,128)(2,1)}, u32[]{:S(2)}, u32[]{:S(2)}) collective-permute-start(bf16[2,384,1536]{2,1,0:T(8,128)(2,1)S(1)} %pad_maximum_fusion.2), channel_id=1, source_target_pairs={{0,16},{1,3},{2,18},{3,1},{4,20},{5,7},{6,22},{7,5},{8,24},{9,11},... | collective-permute-start | bytes 7077896 | tf_op jit(solution)/shard_map/ppermute | solution.py:135
  257.7 13.1 %collective-permute-start.15 = (bf16[192,1152]{1,0:T(8,128)(2,1)S(1)}, bf16[192,1152]{1,0:T(8,128)(2,1)S(1)}, u32[]{:S(2)}, u32[]{:S(2)}) collective-permute-start(bf16[192,1152]{1,0:T(8,128)(2,1)S(1)} %bitcast.403), channel_id=1, source_target_pairs={{0,2},{1,3},{2,0},{3,1},{4,6},{5,7},{6,4},{7,5},{8,10},{9,11},{10,... | collective-permute-start | bytes 1327112 | tf_op jit(solution)/shard_map/ppermute | solution.py:135
  262.0 45.6 %collective-permute-start.8 = (bf16[384,1536]{1,0:T(8,128)(2,1)S(1)}, bf16[384,1536]{1,0:T(8,128)(2,1)S(1)}, u32[]{:S(2)}, u32[]{:S(2)}) collective-permute-start(bf16[384,1536]{1,0:T(8,128)(2,1)S(1)} %get-tuple-element.25), channel_id=1, source_target_pairs={{0,2},{1,17},{2,0},{3,19},{4,6},{5,21},{6,4},{7,23},{8,10},{9,25},... | collective-permute-start | bytes 3538952 | tf_op jit(solution)/shard_map/ppermute | solution.py:135
  264.0 52.6 %collective-permute-start.22 = (bf16[384,1536]{1,0:T(8,128)(2,1)}, bf16[384,1536]{1,0:T(8,128)(2,1)S(1)}, u32[]{:S(2)}, u32[]{:S(2)}) collective-permute-start(bf16[384,1536]{1,0:T(8,128)(2,1)} %bitcast.49), channel_id=1, source_target_pairs={{0,1},{1,0},{2,3},{3,2},{4,5},{5,4},{6,7},{7,6},{8,9},{9,8},{10,11... | collective-permute-start | bytes 3538952 | tf_op jit(solution)/shard_map/ppermute | solution.py:135
  297.6 21.2 %collective-permute-start.24 = (bf16[2,384,1536]{2,1,0:T(8,128)(2,1)}, bf16[2,384,1536]{2,1,0:T(8,128)(2,1)}, u32[]{:S(2)}, u32[]{:S(2)}) collective-permute-start(bf16[2,384,1536]{2,1,0:T(8,128)(2,1)} %collective-permute-done.21), channel_id=1, source_target_pairs={{0,1},{1,0},{2,3},{3,2},{4,5},{5,4},{6,7},{7,6},{8,9},{9,8},{10,11... | collective-permute-start | bytes 7077896 | tf_op jit(solution)/shard_map/ppermute | solution.py:135
  307.4 240.5 %reduce-scatter.14.cloned.1.call-start = ((), (), s32[]{:S(2)}) async-start(), calls=%async_computation.10 | async-start | bytes 4423680 | tf_op jit(solution)/shard_map/reduce_scatter | solution.py:182
  307.5 10.2 %collective-permute-start.23 = (bf16[384,1536]{1,0:T(8,128)(2,1)}, bf16[384,1536]{1,0:T(8,128)(2,1)S(1)}, u32[]{:S(2)}, u32[]{:S(2)}) collective-permute-start(bf16[384,1536]{1,0:T(8,128)(2,1)} %collective-permute-done.20), channel_id=1, source_target_pairs={{0,1},{1,0},{2,3},{3,2},{4,5},{5,4},{6,7},{7,6},{8,9},{9,8},{10,11... | collective-permute-start | bytes 3538952 | tf_op jit(solution)/shard_map/ppermute | solution.py:135
  307.8 28.9 %collective-permute-start.9 = (bf16[2,384,1536]{2,1,0:T(8,128)(2,1)S(1)}, bf16[2,384,1536]{2,1,0:T(8,128)(2,1)S(1)}, u32[]{:S(2)}, u32[]{:S(2)}) collective-permute-start(bf16[2,384,1536]{2,1,0:T(8,128)(2,1)S(1)} %pad_maximum_fusion), channel_id=1, source_target_pairs={{0,16},{1,3},{2,18},{3,1},{4,20},{5,7},{6,22},{7,5},{8,24},{9,11},... | collective-permute-start | bytes 7077896 | tf_op jit(solution)/shard_map/ppermute | solution.py:135
  318.8 24.2 %collective-permute-start.10 = (bf16[384,1536]{1,0:T(8,128)(2,1)S(1)}, bf16[384,1536]{1,0:T(8,128)(2,1)S(1)}, u32[]{:S(2)}, u32[]{:S(2)}) collective-permute-start(bf16[384,1536]{1,0:T(8,128)(2,1)S(1)} %get-tuple-element.25), channel_id=1, source_target_pairs={{0,1},{1,0},{2,3},{3,2},{4,5},{5,4},{6,7},{7,6},{8,9},{9,8},{10,11... | collective-permute-start | bytes 3538952 | tf_op jit(solution)/shard_map/ppermute | solution.py:135
  336.7 8.5 collective-permute-start.12
  339.1 5.0 collective-permute-start.11
  438.1 141.4 %reduce-scatter.12.cloned.1.call-start = ((), (), s32[]{:S(2)}) async-start(), calls=%async_computation.9 | async-start | bytes 4423680 | tf_op jit(solution)/shard_map/reduce_scatter | solution.py:182
  456.2 192.4 %reduce-scatter.10.cloned.1.call-start = ((), (), s32[]{:S(2)}) async-start(), calls=%async_computation.8 | async-start | bytes 4423680 | tf_op jit(solution)/shard_map/reduce_scatter | solution.py:182
  467.6 49.7 %collective-permute-start.16 = (bf16[1536,1536]{1,0:T(8,128)(2,1)}, bf16[1536,1536]{1,0:T(8,128)(2,1)}, u32[]{:S(2)}, u32[]{:S(2)}) collective-permute-start(bf16[1536,1536]{1,0:T(8,128)(2,1)} %convolution_convert_fusion), channel_id=1, source_target_pairs={{0,1},{1,0},{2,3},{3,2},{4,5},{5,4},{6,7},{7,6},{8,9},{9,8},{10,11... | collective-permute-start | bytes 14155784 | tf_op jit(solution)/shard_map/ppermute | solution.py:135
  490.4 39.0 %collective-permute-start.25 = (bf16[1536,1536]{1,0:T(8,128)(2,1)}, bf16[1536,1536]{1,0:T(8,128)(2,1)}, u32[]{:S(2)}, u32[]{:S(2)}) collective-permute-start(bf16[1536,1536]{1,0:T(8,128)(2,1)} %add_convert_fusion), channel_id=1, source_target_pairs={{0,1},{1,0},{2,3},{3,2},{4,5},{5,4},{6,7},{7,6},{8,9},{9,8},{10,11... | collective-permute-start | bytes 14155784 | tf_op jit(solution)/shard_map/ppermute | solution.py:135
  505.4 318.9 %reduce-scatter.8.cloned.1.call-start = ((), (), s32[]{:S(2)}) async-start(), calls=%async_computation.7 | async-start | bytes 2654208 | tf_op jit(solution)/shard_map/reduce_scatter | solution.py:192
  528.2 122.9 %collective-permute-start.17 = (bf16[2,384,1536]{2,1,0:T(8,128)(2,1)}, bf16[2,384,1536]{2,1,0:T(8,128)(2,1)}, u32[]{:S(2)}, u32[]{:S(2)}) collective-permute-start(bf16[2,384,1536]{2,1,0:T(8,128)(2,1)} %bitcast.45), channel_id=1, source_target_pairs={{0,16},{1,3},{2,18},{3,1},{4,20},{5,7},{6,22},{7,5},{8,24},{9,11},... | collective-permute-start | bytes 7077896 | tf_op jit(solution)/shard_map/ppermute | solution.py:135
  543.9 112.1 %collective-permute-start.26 = (bf16[2,384,1536]{2,1,0:T(8,128)(2,1)}, bf16[2,384,1536]{2,1,0:T(8,128)(2,1)}, u32[]{:S(2)}, u32[]{:S(2)}) collective-permute-start(bf16[2,384,1536]{2,1,0:T(8,128)(2,1)} %bitcast.56), channel_id=1, source_target_pairs={{0,16},{1,3},{2,18},{3,1},{4,20},{5,7},{6,22},{7,5},{8,24},{9,11},... | collective-permute-start | bytes 7077896 | tf_op jit(solution)/shard_map/ppermute | solution.py:135
  549.0 111.1 %collective-permute-start.42 = (bf16[192,1152]{1,0:T(8,128)(2,1)S(1)}, bf16[192,1152]{1,0:T(8,128)(2,1)S(1)}, u32[]{:S(2)}, u32[]{:S(2)}) collective-permute-start(bf16[192,1152]{1,0:T(8,128)(2,1)S(1)} %dynamic-slice_bitcast_fusion), channel_id=1, source_target_pairs={{0,2},{1,3},{2,0},{3,1},{4,6},{5,7},{6,4},{7,5},{8,10},{9,11},{10,... | collective-permute-start | bytes 1327112 | tf_op jit(solution)/shard_map/ppermute | solution.py:135
  580.6 81.3 %collective-permute-start.40 = (bf16[192,1152]{1,0:T(8,128)(2,1)S(1)}, bf16[192,1152]{1,0:T(8,128)(2,1)S(1)}, u32[]{:S(2)}, u32[]{:S(2)}) collective-permute-start(bf16[192,1152]{1,0:T(8,128)(2,1)S(1)} %dynamic-slice_bitcast_fusion.1), channel_id=1, source_target_pairs={{0,2},{1,3},{2,0},{3,1},{4,6},{5,7},{6,4},{7,5},{8,10},{9,11},{10,... | collective-permute-start | bytes 1327112 | tf_op jit(solution)/shard_map/ppermute | solution.py:135
  649.6 13.1 %collective-permute-start.38 = (bf16[192,1152]{1,0:T(8,128)(2,1)S(1)}, bf16[192,1152]{1,0:T(8,128)(2,1)S(1)}, u32[]{:S(2)}, u32[]{:S(2)}) collective-permute-start(bf16[192,1152]{1,0:T(8,128)(2,1)S(1)} %dynamic-slice_bitcast_fusion.2), channel_id=1, source_target_pairs={{0,2},{1,3},{2,0},{3,1},{4,6},{5,7},{6,4},{7,5},{8,10},{9,11},{10,... | collective-permute-start | bytes 1327112 | tf_op jit(solution)/shard_map/ppermute | solution.py:135
  655.3 31.9 %collective-permute-start.18 = (bf16[384,1536]{1,0:T(8,128)(2,1)S(1)}, bf16[384,1536]{1,0:T(8,128)(2,1)S(1)}, u32[]{:S(2)}, u32[]{:S(2)}) collective-permute-start(bf16[384,1536]{1,0:T(8,128)(2,1)S(1)} %fusion.54), channel_id=1, source_target_pairs={{0,2},{1,17},{2,0},{3,19},{4,6},{5,21},{6,4},{7,23},{8,10},{9,25},... | collective-permute-start | bytes 3538952 | tf_op jit(solution)/shard_map/ppermute | solution.py:135
  658.6 27.9 %collective-permute-start.27 = (bf16[384,1536]{1,0:T(8,128)(2,1)S(1)}, bf16[384,1536]{1,0:T(8,128)(2,1)S(1)}, u32[]{:S(2)}, u32[]{:S(2)}) collective-permute-start(bf16[384,1536]{1,0:T(8,128)(2,1)S(1)} %fusion.55), channel_id=1, source_target_pairs={{0,2},{1,17},{2,0},{3,19},{4,6},{5,21},{6,4},{7,23},{8,10},{9,25},... | collective-permute-start | bytes 3538952 | tf_op jit(solution)/shard_map/ppermute | solution.py:135
  660.3 44.9 %collective-permute-start.43 = (bf16[2,192,1152]{2,1,0:T(8,128)(2,1)S(1)}, bf16[2,192,1152]{2,1,0:T(8,128)(2,1)}, u32[]{:S(2)}, u32[]{:S(2)}) collective-permute-start(bf16[2,192,1152]{2,1,0:T(8,128)(2,1)S(1)} %pad_maximum_fusion.23), channel_id=1, source_target_pairs={{0,16},{1,17},{2,18},{3,19},{4,20},{5,21},{6,22},{7,23},{8,24},{9,... | collective-permute-start | bytes 2654216 | tf_op jit(solution)/shard_map/ppermute | solution.py:135
  662.1 44.7 %collective-permute-start.41 = (bf16[2,192,1152]{2,1,0:T(8,128)(2,1)S(1)}, bf16[2,192,1152]{2,1,0:T(8,128)(2,1)}, u32[]{:S(2)}, u32[]{:S(2)}) collective-permute-start(bf16[2,192,1152]{2,1,0:T(8,128)(2,1)S(1)} %pad_maximum_fusion.22), channel_id=1, source_target_pairs={{0,16},{1,17},{2,18},{3,19},{4,20},{5,21},{6,22},{7,23},{8,24},{9,... | collective-permute-start | bytes 2654216 | tf_op jit(solution)/shard_map/ppermute | solution.py:135
  662.9 58.0 %collective-permute-start.39 = (bf16[2,192,1152]{2,1,0:T(8,128)(2,1)S(1)}, bf16[2,192,1152]{2,1,0:T(8,128)(2,1)S(1)}, u32[]{:S(2)}, u32[]{:S(2)}) collective-permute-start(bf16[2,192,1152]{2,1,0:T(8,128)(2,1)S(1)} %pad_maximum_fusion.21), channel_id=1, source_target_pairs={{0,16},{1,17},{2,18},{3,19},{4,20},{5,21},{6,22},{7,23},{8,24},{9,... | collective-permute-start | bytes 2654216 | tf_op jit(solution)/shard_map/ppermute | solution.py:135
  690.6 32.6 %collective-permute-start.28 = (bf16[384,1536]{1,0:T(8,128)(2,1)S(1)}, bf16[384,1536]{1,0:T(8,128)(2,1)S(1)}, u32[]{:S(2)}, u32[]{:S(2)}) collective-permute-start(bf16[384,1536]{1,0:T(8,128)(2,1)S(1)} %get-tuple-element.20), channel_id=1, source_target_pairs={{0,1},{1,0},{2,3},{3,2},{4,5},{5,4},{6,7},{7,6},{8,9},{9,8},{10,11... | collective-permute-start | bytes 3538952 | tf_op jit(solution)/shard_map/ppermute | solution.py:135
  705.2 101.3 %collective-permute-start.19 = (bf16[384,1536]{1,0:T(8,128)(2,1)}, bf16[384,1536]{1,0:T(8,128)(2,1)}, u32[]{:S(2)}, u32[]{:S(2)}) collective-permute-start(bf16[384,1536]{1,0:T(8,128)(2,1)} %get-tuple-element.37), channel_id=1, source_target_pairs={{0,1},{1,0},{2,3},{3,2},{4,5},{5,4},{6,7},{7,6},{8,9},{9,8},{10,11... | collective-permute-start | bytes 3538952 | tf_op jit(solution)/shard_map/ppermute | solution.py:135
  728.4 164.7 %reduce-scatter.6.cloned.1.call-start = ((), (), s32[]{:S(2)}) async-start(), calls=%async_computation.6 | async-start | bytes 3538944 | tf_op jit(solution)/shard_map/reduce_scatter | solution.py:192
  783.2 21.0 %collective-permute-start.29 = (bf16[384,1536]{1,0:T(8,128)(2,1)S(1)}, bf16[384,1536]{1,0:T(8,128)(2,1)S(1)}, u32[]{:S(2)}, u32[]{:S(2)}) collective-permute-start(bf16[384,1536]{1,0:T(8,128)(2,1)S(1)} %fusion.53), channel_id=1, source_target_pairs={{0,1},{1,0},{2,3},{3,2},{4,5},{5,4},{6,7},{7,6},{8,9},{9,8},{10,11... | collective-permute-start | bytes 3538952 | tf_op jit(solution)/shard_map/ppermute | solution.py:135
  815.9 7.0 collective-permute-start.30
  816.3 4.7 collective-permute-start.34
  824.4 71.8 %collective-permute-start.37 = (bf16[192,768]{1,0:T(8,128)(2,1)}, bf16[192,768]{1,0:T(8,128)(2,1)S(1)}, u32[]{:S(2)}, u32[]{:S(2)}) collective-permute-start(bf16[192,768]{1,0:T(8,128)(2,1)} %reduce-scatter.8.cloned.1.call-done), channel_id=1, source_target_pairs={{0,16},{1,17},{2,18},{3,19},{4,20},{5,21},{6,22},{7,23},{8,24},{9,... | collective-permute-start | bytes 884744 | tf_op jit(solution)/shard_map/ppermute | solution.py:135
  893.1 10.5 %collective-permute-start.36 = (bf16[192,1024]{1,0:T(8,128)(2,1)}, bf16[192,1024]{1,0:T(8,128)(2,1)S(1)}, u32[]{:S(2)}, u32[]{:S(2)}) collective-permute-start(bf16[192,1024]{1,0:T(8,128)(2,1)} %reduce-scatter.6.cloned.1.call-done), channel_id=1, source_target_pairs={{0,16},{1,17},{2,18},{3,19},{4,20},{5,21},{6,22},{7,23},{8,24},{9,... | collective-permute-start | bytes 1179656 | tf_op jit(solution)/shard_map/ppermute | solution.py:135
  (87 other events, 1199.7 us)
Sparse Core Ops, SparseCore 0:
  10.2 86.3 all-gather.7
  98.2 76.0 all-gather.11
  176.4 76.4 all-gather.9
  307.6 82.7 all-gather.13
  438.3 72.3 reduce-scatter.13
  512.8 66.6 reduce-scatter.11
  581.8 66.6 reduce-scatter.9
  728.5 87.1 reduce-scatter.7
  819.2 73.7 reduce-scatter.5
